TPU v7x, 512 devices: a whole 4x8x8 slice. The times are simulated.
512 devices in a mesh: gx: 8 (over z), gy: 8 (over x, core), gz: 8 (over y).
Axes of the slice: x: 4, y: 8, z: 8, core: 2. Of those that a mesh axis runs over, the one named last changes fastest.
Arguments:
- phase_mask: int32 [128, 256, 1024], P('gx', 'gy', 'gz'), may hold values from 0 to 2
- pressure: float32 [128, 256, 1024], P('gx', 'gy', 'gz'), may hold values from -6 to 6
- velocity_cot: float32 [3, 128, 256, 1024], P(None, 'gx', 'gy', 'gz'), may hold values from -30 to 30
Outputs:
- ustar_cot: float32 [3, 128, 256, 1024], P(None, 'gx', 'gy', 'gz')
- coef_cot: float32 [128, 256, 1024], P('gx', 'gy', 'gz')
Inputs may be any that keep to these rules, and one draw needn't show every extreme that they name: `phase_mask`: 0 air, 1 water, 2 interface band.
All inputs are finite; a program needn't handle non-finite values.
Results may differ from a plain program's by a relative error of at most 0.0001.
Values sent between devices are 32-bit elements; how exact they have to be, the bound alone decides.
A program may use at most 64 MiB of HBM per device.

v0:
```python
import jax
import jax.numpy as jnp
from jax import lax
from jax.sharding import PartitionSpec as P

ITERS = 3


def extended(cells, sides, width):
    for axis, dim in sides:
        count = lax.axis_size(axis)
        ends = count - 1
        head = lax.slice_in_dim(cells, 0, width, axis=dim)
        tail = lax.slice_in_dim(cells, cells.shape[dim] - width, cells.shape[dim], axis=dim)
        cells = jnp.concatenate(
            [
                lax.ppermute(tail, axis, [(i, (i + 1) % count) for i in range(ends)]),
                cells,
                lax.ppermute(head, axis, [((i + 1) % count, i) for i in range(ends)]),
            ],
            axis=dim,
        )
    return cells


def coefficient(phase_mask):
    return jnp.where(phase_mask == 0, 8.0, jnp.where(phase_mask == 1, 1.0, 2.0)).astype(jnp.float32)


def face_pair(padded, dim_idx):
    count = padded.shape[dim_idx]
    lower = lax.slice_in_dim(padded, 0, count - 1, axis=dim_idx)
    upper = lax.slice_in_dim(padded, 1, count, axis=dim_idx)
    for other in range(3):
        if other != dim_idx:
            width = padded.shape[other]
            lower = lax.slice_in_dim(lower, 1, width - 1, axis=other)
            upper = lax.slice_in_dim(upper, 1, width - 1, axis=other)
    return (upper, lower)


def face_grads(padded):
    result = []
    for dim_idx in range(3):
        upper, lower = face_pair(padded, dim_idx)
        result.append(upper - lower)
    return tuple(result)


def face_weights(coef_padded):
    result = []
    for dim_idx in range(3):
        upper, lower = face_pair(coef_padded, dim_idx)
        result.append(0.5 * (upper + lower))
    return tuple(result)


def diverge(fluxes):
    total = None
    for dim_idx in range(3):
        flux = fluxes[dim_idx]
        count = flux.shape[dim_idx]
        term = lax.slice_in_dim(flux, 0, count - 1, axis=dim_idx) - lax.slice_in_dim(
            flux, 1, count, axis=dim_idx
        )
        total = term if total is None else total + term
    return total


def spread(fluxes):
    total = None
    for dim_idx in range(3):
        flux = fluxes[dim_idx]
        count = flux.shape[dim_idx]
        term = lax.slice_in_dim(flux, 0, count - 1, axis=dim_idx) + lax.slice_in_dim(
            flux, 1, count, axis=dim_idx
        )
        total = term if total is None else total + term
    return total


def extend(field):
    return extended(field, (("gx", 0), ("gy", 1), ("gz", 2)), 1)


def operate(field, weights):
    grads = face_grads(extend(field))
    return diverge(tuple((weights[dim_idx] * grads[dim_idx] for dim_idx in range(3))))


def norm_sum(resid, precd):
    return lax.psum(jnp.sum(resid * precd), ("gx", "gy", "gz"))


def on_device(phase_mask, pressure, velocity_cot):
    coef_cells = coefficient(phase_mask)
    stacked = jnp.concatenate([coef_cells[None], pressure[None], velocity_cot], 0)
    padded = extended(stacked, (("gx", 1), ("gy", 2), ("gz", 3)), 1)
    coef_padded = padded[0]
    press_padded = padded[1]
    vel_faces = tuple((face_pair(padded[2 + dim_idx], dim_idx)[1] for dim_idx in range(3)))
    weights = face_weights(coef_padded)
    precond = 1.0 / spread(weights)
    rhs = -diverge(tuple((weights[dim_idx] * vel_faces[dim_idx] for dim_idx in range(3))))
    press_grads = face_grads(press_padded)
    solution = jnp.zeros_like(rhs)
    resid = rhs
    precd = precond * resid
    direction = precd
    rz_now = norm_sum(resid, precd)
    for iteration in range(ITERS):
        image = operate(direction, weights)
        step_len = rz_now / lax.psum(jnp.sum(direction * image), ("gx", "gy", "gz"))
        solution = solution + step_len * direction
        resid = resid - step_len * image
        if iteration + 1 < ITERS:
            precd = precond * resid
            rz_next = norm_sum(resid, precd)
            direction = precd + rz_next / rz_now * direction
            rz_now = rz_next
    lam_grads = face_grads(extend(solution))
    columns = []
    for dim_idx in range(3):
        count = lam_grads[dim_idx].shape[dim_idx]
        columns.append(
            velocity_cot[dim_idx] + lax.slice_in_dim(lam_grads[dim_idx], 1, count, axis=dim_idx)
        )
    ustar_cot = jnp.stack(columns, 0)
    wbar = tuple(
        (-press_grads[dim_idx] * (vel_faces[dim_idx] + lam_grads[dim_idx]) for dim_idx in range(3))
    )
    coef_cot = 0.5 * spread(wbar)
    return (ustar_cot, coef_cot)


def solution(mesh):
    in_specs = (P("gx", "gy", "gz"), P("gx", "gy", "gz"), P(None, "gx", "gy", "gz"))
    out_specs = (P(None, "gx", "gy", "gz"), P("gx", "gy", "gz"))
    return jax.shard_map(
        on_device, mesh=mesh, in_specs=in_specs, out_specs=out_specs, check_vma=False
    )
```

profile of v0, /device:TPU:1, one launch (start us, length us, event | category | flops | bytes accessed | tf_op | source)
XLA Modules:
  0.0 678.2 jit_solution(1298808492264359766)
XLA Ops:
  2.6 4.8 collective-permute-start
  8.9 4.4 collective-permute-done.1
  13.3 4.8 collective-permute-start.2
  20.4 3.2 collective-permute-done.3
  27.9 3.2 collective-permute-start.4
  34.5 3.0 collective-permute-done.5
  37.5 2.8 copy.17
  40.3 5.5 pad_maximum_fusion
  50.5 4.6 collective-permute-start.7
  57.9 4.3 collective-permute-start.9
  64.5 4.0 collective-permute-start.11
  68.6 5.5 collective-permute-done.10
  77.6 107.8 %all-reduce = (f32[]{:T(128)}, f32[]{:T(128)}) all-reduce(f32[]{:T(128)} %get-tuple-element.5, f32[]{:T(128)} %get-tuple-element.4), channel_id=1, replica_groups=mesh['gx'=8,'gy'=8,'gz'=8] {'gx','gy','gz'}, use_global_device_ids=true, to_apply=%region_1.2 | all-reduce | flops 2 | bytes 16 | tf_op jit(solution)/shard_map/psum | solution.py:92
  189.1 95.2 %psum.44 = f32[]{:T(128)} all-reduce(f32[]{:T(128)} %get-tuple-element.14), channel_id=1, replica_groups=mesh['gx'=8,'gy'=8,'gz'=8] {'gx','gy','gz'}, use_global_device_ids=true, to_apply=%region_5.6 | all-reduce | flops 1 | bytes 8 | tf_op jit(solution)/shard_map/psum | solution.py:92
  287.9 4.5 collective-permute-start.13
  293.3 3.4 collective-permute-start.14
  296.7 3.5 collective-permute-start.15
  302.5 4.3 collective-permute-start.17
  306.9 6.0 collective-permute-done.16
  316.3 99.8 %psum.45 = f32[]{:T(128)} all-reduce(f32[]{:T(128)} %get-tuple-element.12), channel_id=1, replica_groups=mesh['gx'=8,'gy'=8,'gz'=8] {'gx','gy','gz'}, use_global_device_ids=true, to_apply=%region_7.8 | all-reduce | flops 1 | bytes 8 | tf_op jit(solution)/shard_map/psum | solution.py:113
  419.2 96.1 %psum.46 = f32[]{:T(128)} all-reduce(f32[]{:T(128)} %multiply_reduce_fusion), channel_id=1, replica_groups=mesh['gx'=8,'gy'=8,'gz'=8] {'gx','gy','gz'}, use_global_device_ids=true, to_apply=%region_9.10 | all-reduce | flops 1 | bytes 8 | tf_op jit(solution)/shard_map/psum | solution.py:92
  519.0 4.0 collective-permute-start.19
  523.9 3.7 collective-permute-start.20
  527.6 2.7 collective-permute-start.21
  532.6 4.1 collective-permute-start.23
  536.7 7.0 %collective-permute-done.22 = f32[18,34,1]{2,1,0:T(8,128)S(1)} collective-permute-done((f32[18,34,1]{2,1,0:T(8,128)S(1)}, f32[18,34,1]{2,1,0:T(8,128)S(1)}, u32[]{:S(2)}, u32[]{:S(2)}) %collective-permute-start.22) | collective-permute-done | bytes 2480 | tf_op jit(solution)/shard_map/ppermute | solution.py:19
  545.6 99.8 %psum.47 = f32[]{:T(128)} all-reduce(f32[]{:T(128)} %fusion.34), channel_id=1, replica_groups=mesh['gx'=8,'gy'=8,'gz'=8] {'gx','gy','gz'}, use_global_device_ids=true, to_apply=%region_11.12 | all-reduce | flops 1 | bytes 8 | tf_op jit(solution)/shard_map/psum | solution.py:113
  648.1 4.0 collective-permute-start.25
  653.0 3.7 collective-permute-start.26
  656.7 3.6 collective-permute-start.27
  663.8 4.0 collective-permute-start.29
  669.2 4.8 collective-permute-done.28
  (102 shorter events, 58.6 us)
Async XLA Ops:
  2.6 6.3 collective-permute-start
  7.4 5.8 collective-permute-start.1
  13.3 7.0 %collective-permute-start.2 = (f32[5,18,1,128]{3,2,1,0:T(1,128)S(1)}, f32[5,18,1,128]{3,2,1,0:T(1,128)S(1)}, u32[]{:S(2)}, u32[]{:S(2)}) collective-permute-start(f32[5,18,1,128]{3,2,1,0:T(1,128)S(1)} %get-tuple-element.38), channel_id=1, source_target_pairs={{0,8},{8,16},{16,24},{24,32},{32,40},{40,48},{48,56},{1,9},{9,17},... | collective-permute-start | bytes 138248 | tf_op jit(solution)/shard_map/ppermute | solution.py:17
  18.1 5.4 collective-permute-start.3
  27.9 5.8 collective-permute-start.4
  32.4 5.1 collective-permute-start.5
  49.1 368.3 %copy-start.4 = (f32[16,32,128]{2,1,0:T(8,128)}, f32[16,32,128]{2,1,0:T(8,128)S(1)}, u32[]{:S(2)}) copy-start(f32[16,32,128]{2,1,0:T(8,128)S(1)} %get-tuple-element.20) | copy-start | bytes 786436
  49.2 5.9 collective-permute-start.6
  50.5 5.5 collective-permute-start.7
  56.0 6.3 collective-permute-start.8
  57.9 5.1 collective-permute-start.9
  63.2 10.8 %collective-permute-start.10 = (f32[18,34,1]{2,1,0:T(8,128)S(1)}, f32[18,34,1]{2,1,0:T(8,128)S(1)}, u32[]{:S(2)}, u32[]{:S(2)}) collective-permute-start(f32[18,34,1]{2,1,0:T(8,128)S(1)} %get-tuple-element.51), channel_id=1, source_target_pairs={{1,0},{2,1},{3,2},{4,3},{5,4},{6,5},{7,6},{9,8},{10,9},{11,10},{12... | collective-permute-start | bytes 7352 | tf_op jit(solution)/shard_map/ppermute | solution.py:19
  64.5 11.3 %collective-permute-start.11 = (f32[18,34,1]{2,1,0:T(8,128)S(1)}, f32[18,34,1]{2,1,0:T(8,128)S(1)}, u32[]{:S(2)}, u32[]{:S(2)}) collective-permute-start(f32[18,34,1]{2,1,0:T(8,128)S(1)} %get-tuple-element.52), channel_id=1, source_target_pairs={{0,1},{1,2},{2,3},{3,4},{4,5},{5,6},{6,7},{8,9},{9,10},{10,11},{11... | collective-permute-start | bytes 7352 | tf_op jit(solution)/shard_map/ppermute | solution.py:17
  286.6 5.8 collective-permute-start.12
  287.9 5.3 collective-permute-start.13
  293.3 7.0 %collective-permute-start.14 = (f32[18,1,128]{2,1,0:T(1,128)S(1)}, f32[18,1,128]{2,1,0:T(1,128)S(1)}, u32[]{:S(2)}, u32[]{:S(2)}) collective-permute-start(f32[18,1,128]{2,1,0:T(1,128)S(1)} %get-tuple-element.60), channel_id=1, source_target_pairs={{8,0},{16,8},{24,16},{32,24},{40,32},{48,40},{56,48},{9,1},{17,9},... | collective-permute-start | bytes 27656 | tf_op jit(solution)/shard_map/ppermute | solution.py:19
  296.7 4.3 collective-permute-start.15
  301.2 11.6 %collective-permute-start.16 = (f32[18,34,1]{2,1,0:T(8,128)S(1)}, f32[18,34,1]{2,1,0:T(8,128)S(1)}, u32[]{:S(2)}, u32[]{:S(2)}) collective-permute-start(f32[18,34,1]{2,1,0:T(8,128)S(1)} %get-tuple-element.49), channel_id=1, source_target_pairs={{1,0},{2,1},{3,2},{4,3},{5,4},{6,5},{7,6},{9,8},{10,9},{11,10},{12... | collective-permute-start | bytes 7352 | tf_op jit(solution)/shard_map/ppermute | solution.py:19
  302.5 12.1 %collective-permute-start.17 = (f32[18,34,1]{2,1,0:T(8,128)S(1)}, f32[18,34,1]{2,1,0:T(8,128)S(1)}, u32[]{:S(2)}, u32[]{:S(2)}) collective-permute-start(f32[18,34,1]{2,1,0:T(8,128)S(1)} %get-tuple-element.50), channel_id=1, source_target_pairs={{0,1},{1,2},{2,3},{3,4},{4,5},{5,6},{6,7},{8,9},{9,10},{10,11},{11... | collective-permute-start | bytes 7352 | tf_op jit(solution)/shard_map/ppermute | solution.py:17
  517.7 5.3 collective-permute-start.18
  519.0 4.8 collective-permute-start.19
  523.9 6.4 collective-permute-start.20
  527.6 3.4 collective-permute-start.21
  531.3 12.4 %collective-permute-start.22 = (f32[18,34,1]{2,1,0:T(8,128)S(1)}, f32[18,34,1]{2,1,0:T(8,128)S(1)}, u32[]{:S(2)}, u32[]{:S(2)}) collective-permute-start(f32[18,34,1]{2,1,0:T(8,128)S(1)} %get-tuple-element.47), channel_id=1, source_target_pairs={{1,0},{2,1},{3,2},{4,3},{5,4},{6,5},{7,6},{9,8},{10,9},{11,10},{12... | collective-permute-start | bytes 7352 | tf_op jit(solution)/shard_map/ppermute | solution.py:19
  532.6 12.0 %collective-permute-start.23 = (f32[18,34,1]{2,1,0:T(8,128)S(1)}, f32[18,34,1]{2,1,0:T(8,128)S(1)}, u32[]{:S(2)}, u32[]{:S(2)}) collective-permute-start(f32[18,34,1]{2,1,0:T(8,128)S(1)} %get-tuple-element.48), channel_id=1, source_target_pairs={{0,1},{1,2},{2,3},{3,4},{4,5},{5,6},{6,7},{8,9},{9,10},{10,11},{11... | collective-permute-start | bytes 7352 | tf_op jit(solution)/shard_map/ppermute | solution.py:17
  646.8 5.3 collective-permute-start.24
  648.1 4.8 collective-permute-start.25
  653.0 9.1 %collective-permute-start.26 = (f32[18,1,128]{2,1,0:T(1,128)S(1)}, f32[18,1,128]{2,1,0:T(1,128)S(1)}, u32[]{:S(2)}, u32[]{:S(2)}) collective-permute-start(f32[18,1,128]{2,1,0:T(1,128)S(1)} %get-tuple-element.56), channel_id=1, source_target_pairs={{8,0},{16,8},{24,16},{32,24},{40,32},{48,40},{56,48},{9,1},{17,9},... | collective-permute-start | bytes 27656 | tf_op jit(solution)/shard_map/ppermute | solution.py:19
  656.7 5.4 collective-permute-start.27
  662.2 13.6 %copy-start.2 = (f32[18,34,130]{2,1,0:T(8,128)S(1)}, f32[18,34,130]{2,1,0:T(8,128)}, u32[]{:S(2)}) copy-start(f32[18,34,130]{2,1,0:T(8,128)} %copy-done.1) | copy-start | bytes 954724
  662.3 11.6 %collective-permute-start.28 = (f32[18,34,1]{2,1,0:T(8,128)S(1)}, f32[18,34,1]{2,1,0:T(8,128)S(1)}, u32[]{:S(2)}, u32[]{:S(2)}) collective-permute-start(f32[18,34,1]{2,1,0:T(8,128)S(1)} %get-tuple-element.45), channel_id=1, source_target_pairs={{1,0},{2,1},{3,2},{4,3},{5,4},{6,5},{7,6},{9,8},{10,9},{11,10},{12... | collective-permute-start | bytes 7352 | tf_op jit(solution)/shard_map/ppermute | solution.py:19
  663.8 12.0 %collective-permute-start.29 = (f32[18,34,1]{2,1,0:T(8,128)S(1)}, f32[18,34,1]{2,1,0:T(8,128)S(1)}, u32[]{:S(2)}, u32[]{:S(2)}) collective-permute-start(f32[18,34,1]{2,1,0:T(8,128)S(1)} %get-tuple-element.46), channel_id=1, source_target_pairs={{0,1},{1,2},{2,3},{3,4},{4,5},{5,6},{6,7},{8,9},{9,10},{10,11},{11... | collective-permute-start | bytes 7352 | tf_op jit(solution)/shard_map/ppermute | solution.py:17
  (5 other events, 28.6 us)
where the time goes:
time: 681 us; the launch traced here: 678 us
  blocking collectives  499 us (73%)
  starting transfers between devices  88.3 us (13%)
  waiting for transfers between devices  45.6 us (7%)
  other arithmetic  26 us (4%)
  local copies, waits for them, and re-layouts  11.8 us (2%)
  between operations  7.69 us (1%)
    psum x3, blocking collectives, norm_sum(): return lax.psum(jnp.sum(resid * precd), ('gx', 'gy', 'gz'))  299 us
    psum x2, blocking collectives, on_device(): step_len = rz_now / lax.psum(jnp.sum(direction * image), ('gx', 'gy', 'gz'))  200 us
    ppermute x15, starting transfers between devices, extended(): lax.ppermute(tail, axis, [(i, (i + 1) % count) for i in range(ends)])  60.3 us
    ppermute x15, waiting for transfers between devices, extended(): lax.ppermute(head, axis, [((i + 1) % count, i) for i in range(ends)])  33.7 us
    ppermute x15, starting transfers between devices, extended(): lax.ppermute(head, axis, [((i + 1) % count, i) for i in range(ends)])  28 us
  transfers between devices with their start and end apart: 30, of which 19 were waited for; matrix products, arithmetic and copies ran while one was open for 1% of the time, Pallas kernels for 0%

commit v1 on v0

v1 whole, which is shorter than its diff:
```python
import jax
import jax.numpy as jnp
from jax import lax
from jax.experimental import pallas as pl
from jax.experimental.pallas import tpu as pltpu
from jax.sharding import PartitionSpec as P


MESH = pl.DeviceIdType.MESH
AXES = ("gx", "gy", "gz")
RING = 8
NXL, NYL, NZL = 16, 32, 128
TOP = 8
LAST = TOP + NYL - 1
BLOCKS = NYL // 8
F32 = jnp.float32


def two_sum(a, b):
    s = a + b
    t = s - a
    return s, (a - (s - t)) + (b - t)


def split(a):
    c = 4097.0 * a
    hi = c - (c - a)
    return hi, a - hi


def sub_mul(x, c, y):
    p = c * y[0]
    ch, cl = split(c)
    yh, yl = split(y[0])
    err = ((ch * yh - p) + ch * yl + cl * yh) + cl * yl
    s, t = two_sum(x[0], -p)
    t = t + (x[1] - (err + c * y[1]))
    hi = s + t
    return hi, t - (hi - s)


def galerkin(sums):
    g0, g2, h00, h01, h02, h11, h12, h22 = sums
    one = jnp.ones_like(g0[0])
    g1 = sub_mul(h00, one, g0)
    a = h01[0] / h00[0]
    b = h02[0] / h00[0]
    h01p = sub_mul(h01, a, h00)
    h02p = sub_mul(h02, b, h00)
    h11p = sub_mul(sub_mul(h11, a, h01), a, h01p)
    h12p = sub_mul(sub_mul(h12, a, h02), b, h01p)
    h22p = sub_mul(sub_mul(h22, b, h02), b, h02p)
    g1p = sub_mul(g1, a, g0)
    g2p = sub_mul(g2, b, g0)
    ok1 = h11p[0] > 1e-10 * h11[0]
    inv1 = jnp.where(ok1, 1.0 / jnp.where(ok1, h11p[0], 1.0), 0.0)
    c = h12p[0] * inv1
    h12q = sub_mul(h12p, c, h11p)
    h22q = sub_mul(sub_mul(h22p, c, h12p), c, h12q)
    g2q = sub_mul(g2p, c, g1p)
    h02q = h02p[0] - c * h01p[0]
    ok2 = h22q[0] > 1e-10 * h22[0]
    y2 = jnp.where(ok2, g2q[0] / jnp.where(ok2, h22q[0], 1.0), 0.0)
    y1p = (g1p[0] - h12q[0] * y2) * inv1
    y0p = (g0[0] - h01p[0] * y1p - h02q * y2) / h00[0]
    return y0p - a * y1p - (b - c * a) * y2, y1p - c * y2, y2


def roll(x, shift, axis):
    return pltpu.roll(x, shift, axis)


def remote(src, dst, send, recv, device):
    return pltpu.make_async_remote_copy(
        src_ref=src, dst_ref=dst, send_sem=send, recv_sem=recv, device_id=device, device_id_type=MESH
    )


def body(
    mask_hbm, press_hbm, vel_hbm, ustar_hbm, coef_hbm,
    mask, fc, fp, fu0, fu1, fu2, fv0, fv1, fv2,
    wx, wyu, wyd, wzu, wzd, minv, rhs, img,
    grads, bases,
    yup, ydn, yup_in, ydn_in, vyup, vydn, vyup_in, vydn_in,
    zup, zin_lo, zin_hi, zmix, vz, vz_lo, vz_hi, vmix,
    sums, out_u, out_c,
    load_sem, store_sem,
    send1, recv1, sendv, recvv, sendr, recvr,
):
    pos = {axis: lax.axis_index(axis) for axis in AXES}
    fwd = {axis: lax.rem(pos[axis] + 1, RING) for axis in AXES}
    bwd = {axis: lax.rem(pos[axis] + RING - 1, RING) for axis in AXES}
    lane = lax.broadcasted_iota(jnp.int32, (8, NZL), 1)
    half = lane // 2
    even = lane - 2 * half == 0
    first = lane == 0
    final = lane == NZL - 1

    cells = (pl.ds(1, NXL), pl.ds(TOP, NYL))
    loads = [pltpu.make_async_copy(mask_hbm, mask, load_sem.at[0])]
    for i, field in enumerate((fu0, fu1, fu2)):
        loads.append(pltpu.make_async_copy(vel_hbm.at[i], field.at[cells], load_sem.at[1 + i]))
    loads.append(pltpu.make_async_copy(press_hbm, fp.at[cells], load_sem.at[4]))
    for load in loads:
        load.start()

    barrier = pltpu.get_barrier_semaphore()
    for axis in AXES:
        for other in (fwd[axis], bwd[axis]):
            pl.semaphore_signal(barrier, inc=1, device_id={axis: other}, device_id_type=MESH)
    for load in loads:
        load.wait()

    def pick(x, k, value, packed):
        return jnp.where(half == BLOCKS * x + k, roll(value, 2 * BLOCKS * x + 2 * k + 1, 1), packed)

    def place(x, k, mixed):
        return roll(mixed, NZL - 1 - 2 * BLOCKS * x - 2 * k, 1)

    def above(value, edge):
        return jnp.where(final, edge, roll(value, NZL - 1, 1))

    def below(value, edge):
        return jnp.where(first, edge, roll(value, 1, 1))

    zero = jnp.zeros((8, NZL), F32)

    def prepare(x, carry):
        pc, pp, pu = carry
        for k in range(BLOCKS):
            rows = pl.ds(TOP + 8 * k, 8)
            phase = mask[x, pl.ds(8 * k, 8)]
            c = jnp.where(phase == 0, 8.0, jnp.where(phase == 1, 1.0, 2.0)).astype(F32)
            fc[x + 1, rows] = c
            pc = pick(x, k, c, pc)
            pp = pick(x, k, fp[x + 1, rows], pp)
            pu = pick(x, k, fu2[x + 1, rows], pu)
            if k == 0:
                ydn[0, pl.ds(x, 1)] = c[0:1]
                ydn[1, pl.ds(x, 1)] = fp[x + 1, pl.ds(TOP, 1)]
            if k == BLOCKS - 1:
                yup[0, pl.ds(x, 1)] = c[7:8]
                yup[1, pl.ds(x, 1)] = fp[x + 1, pl.ds(LAST, 1)]
                yup[2, pl.ds(x, 1)] = fu1[x + 1, pl.ds(LAST, 1)]
        return pc, pp, pu

    pc, pp, pu = lax.fori_loop(0, NXL, prepare, (zero, zero, zero), unroll=4)
    zup[0] = pc
    zup[1] = pp
    zup[2] = pu

    pl.semaphore_wait(barrier, 6)

    inner = pl.ds(TOP, NYL)
    round1 = [
        remote(fc.at[NXL, inner], fc.at[0, inner], send1.at[0], recv1.at[0], {"gx": fwd["gx"]}),
        remote(fc.at[1, inner], fc.at[NXL + 1, inner], send1.at[1], recv1.at[1], {"gx": bwd["gx"]}),
        remote(fu0.at[NXL, inner], fu0.at[0, inner], send1.at[2], recv1.at[2], {"gx": fwd["gx"]}),
        remote(fp.at[NXL, inner], fp.at[0, inner], send1.at[3], recv1.at[3], {"gx": fwd["gx"]}),
        remote(fp.at[1, inner], fp.at[NXL + 1, inner], send1.at[4], recv1.at[4], {"gx": bwd["gx"]}),
        remote(yup, yup_in, send1.at[5], recv1.at[5], {"gy": fwd["gy"]}),
        remote(ydn, ydn_in, send1.at[6], recv1.at[6], {"gy": bwd["gy"]}),
        remote(zup, zin_lo, send1.at[7], recv1.at[7], {"gz": fwd["gz"]}),
        remote(zup, zin_hi, send1.at[8], recv1.at[8], {"gz": bwd["gz"]}),
    ]
    for copy in round1:
        copy.start()
    for copy in round1:
        copy.wait_recv()

    low = {axis: pos[axis] == 0 for axis in AXES}
    high = {axis: pos[axis] == RING - 1 for axis in AXES}

    def clear_x(fields_low, fields_high):
        @pl.when(low["gx"])
        def _():
            for field in fields_low:
                field[0, inner] = jnp.zeros((NYL, NZL), F32)

        @pl.when(high["gx"])
        def _():
            for field in fields_high:
                field[NXL + 1, inner] = jnp.zeros((NYL, NZL), F32)

    def mix(lo, hi):
        lo = jnp.where(low["gz"], 0.0, lo)
        hi = jnp.where(high["gz"], 0.0, hi)
        return jnp.where(even, roll(hi, NZL - 1, 1), roll(lo, 1, 1))

    clear_x((fc, fp, fu0), (fc, fp))
    for i in range(3):
        zmix[i] = mix(zin_lo[i], zin_hi[i])
    for x in range(NXL):
        row = pl.ds(x, 1)
        fc[x + 1, pl.ds(TOP - 1, 1)] = jnp.where(low["gy"], 0.0, yup_in[0, row])
        fp[x + 1, pl.ds(TOP - 1, 1)] = jnp.where(low["gy"], 0.0, yup_in[1, row])
        fu1[x + 1, pl.ds(TOP - 1, 1)] = jnp.where(low["gy"], 0.0, yup_in[2, row])
        fc[x + 1, pl.ds(LAST + 1, 1)] = jnp.where(high["gy"], 0.0, ydn_in[0, row])
        fp[x + 1, pl.ds(LAST + 1, 1)] = jnp.where(high["gy"], 0.0, ydn_in[1, row])

    wx[0] = 0.5 * (fc[0, inner] + fc[1, inner])

    def faces(x, k, value):
        if k == 0:
            vydn[pl.ds(x, 1)] = value[0:1]
        if k == BLOCKS - 1:
            vyup[pl.ds(x, 1)] = value[7:8]

    def start(x, carry):
        packed, g0 = carry
        for k in range(BLOCKS):
            r = TOP + 8 * k
            rows, own = pl.ds(r, 8), pl.ds(8 * k, 8)
            c = fc[x + 1, rows]
            edge = place(x, k, zmix[0])
            xu = 0.5 * (c + fc[x + 2, rows])
            xd = wx[x, own]
            yu = 0.5 * (c + fc[x + 1, pl.ds(r + 1, 8)])
            yd = 0.5 * (c + fc[x + 1, pl.ds(r - 1, 8)])
            zu = 0.5 * (c + above(c, edge))
            zd = 0.5 * (c + below(c, edge))
            m = 1.0 / ((xd + xu) + (yd + yu) + (zd + zu))
            u2 = fu2[x + 1, rows]
            r0 = (
                (xu * fu0[x + 1, rows] - xd * fu0[x, rows])
                + (yu * fu1[x + 1, rows] - yd * fu1[x + 1, pl.ds(r - 1, 8)])
                + (zu * u2 - zd * below(u2, place(x, k, zmix[2])))
            )
            v = m * r0
            wx[x + 1, own] = xu
            wyu[x, own] = yu
            wyd[x, own] = yd
            wzu[x, own] = zu
            wzd[x, own] = zd
            minv[x, own] = m
            rhs[x, own] = r0
            fv0[x + 1, rows] = v
            packed = pick(x, k, v, packed)
            faces(x, k, v)
            g0 = g0 + v * r0
        return packed, g0

    packed, g0 = lax.fori_loop(0, NXL, start, (zero, zero), unroll=4)

    def exchange(i, field, packed):
        vz[i] = packed
        copies = [
            remote(field.at[NXL, inner], field.at[0, inner], sendv.at[i, 0], recvv.at[i, 0], {"gx": fwd["gx"]}),
            remote(field.at[1, inner], field.at[NXL + 1, inner], sendv.at[i, 1], recvv.at[i, 1], {"gx": bwd["gx"]}),
            remote(vyup, vyup_in.at[i], sendv.at[i, 2], recvv.at[i, 2], {"gy": fwd["gy"]}),
            remote(vydn, vydn_in.at[i], sendv.at[i, 3], recvv.at[i, 3], {"gy": bwd["gy"]}),
            remote(vz.at[i], vz_lo.at[i], sendv.at[i, 4], recvv.at[i, 4], {"gz": fwd["gz"]}),
            remote(vz.at[i], vz_hi.at[i], sendv.at[i, 5], recvv.at[i, 5], {"gz": bwd["gz"]}),
        ]
        for copy in copies:
            copy.start()
        for copy in copies:
            copy.wait()
        clear_x((field,), (field,))
        vmix[i] = mix(vz_lo[i], vz_hi[i])
        for x in range(NXL):
            row = pl.ds(x, 1)
            field[x + 1, pl.ds(TOP - 1, 1)] = jnp.where(low["gy"], 0.0, vyup_in[i, row])
            field[x + 1, pl.ds(LAST + 1, 1)] = jnp.where(high["gy"], 0.0, vydn_in[i, row])

    def around(x, k, i, field):
        r = TOP + 8 * k
        rows = pl.ds(r, 8)
        v = field[x + 1, rows]
        edge = place(x, k, vmix[i])
        return (
            v,
            (field[x + 2, rows], field[x + 1, pl.ds(r + 1, 8)], above(v, edge)),
            (field[x, rows], field[x + 1, pl.ds(r - 1, 8)], below(v, edge)),
        )

    def operate(x, k, i, field):
        own = pl.ds(8 * k, 8)
        v, (xp, yp, zp), (xm, ym, zm) = around(x, k, i, field)
        image = (
            (wx[x, own] * (v - xm) + wx[x + 1, own] * (v - xp))
            + (wyd[x, own] * (v - ym) + wyu[x, own] * (v - yp))
            + (wzd[x, own] * (v - zm) + wzu[x, own] * (v - zp))
        )
        return v, image

    exchange(0, fv0, packed)

    def step0(x, carry):
        packed, h00, h01 = carry
        for k in range(BLOCKS):
            own = pl.ds(8 * k, 8)
            v, q = operate(x, k, 0, fv0)
            w = minv[x, own] * q - v
            img[x, own] = q
            fv1[x + 1, pl.ds(TOP + 8 * k, 8)] = w
            packed = pick(x, k, w, packed)
            faces(x, k, w)
            h00 = h00 + v * q
            h01 = h01 + w * q
        return packed, h00, h01

    packed, h00, h01 = lax.fori_loop(0, NXL, step0, (zero, zero, zero), unroll=4)
    exchange(1, fv1, packed)

    def step1(x, carry):
        packed, h02, h11, h12, g2 = carry
        for k in range(BLOCKS):
            own = pl.ds(8 * k, 8)
            v, q = operate(x, k, 1, fv1)
            w = minv[x, own] * q - v
            fv2[x + 1, pl.ds(TOP + 8 * k, 8)] = w
            packed = pick(x, k, w, packed)
            faces(x, k, w)
            h02 = h02 + w * img[x, own]
            h11 = h11 + v * q
            h12 = h12 + w * q
            g2 = g2 + w * rhs[x, own]
        return packed, h02, h11, h12, g2

    packed, h02, h11, h12, g2 = lax.fori_loop(0, NXL, step1, (zero,) * 5, unroll=4)
    exchange(2, fv2, packed)

    def step2(x, h22):
        for k in range(BLOCKS):
            v, q = operate(x, k, 2, fv2)
            h22 = h22 + v * q
        return h22

    h22 = lax.fori_loop(0, NXL, step2, zero, unroll=4)

    sub = lax.broadcasted_iota(jnp.int32, (8, NZL), 0)
    level = [(value, None) for value in (g0, g2, h00, h01, h02, h11, h12, h22)]
    for width in (4, 2, 1):
        keep = lax.rem(sub // width, 2) == 0
        merged = []
        n = len(level) // 2
        for i in range(n):
            (ah, al), (bh, bl) = level[i], level[i + n]
            hi, err = two_sum(jnp.where(keep, ah, bh), roll_rows(jnp.where(keep, bh, ah), width, keep))
            if al is not None:
                err = err + (jnp.where(keep, al, bl) + roll_rows(jnp.where(keep, bl, al), width, keep))
            merged.append((hi, err))
        level = merged
    hi, lo = level[0]
    for width in (64, 32, 16, 8, 4, 2, 1):
        hi, err = two_sum(hi, roll(hi, width, 1))
        lo = (lo + roll(lo, width, 1)) + err
    own_row = jnp.where(lane == sub, hi, 0.0) + jnp.where(lane == sub + 64, lo, 0.0)
    row = jnp.sum(own_row, axis=0, keepdims=True)

    low_half = lax.broadcasted_iota(jnp.int32, (1, NZL), 1) < 64

    for phase, axis in enumerate(("gy", "gx", "gz")):
        slots = sums.at[phase]
        sums[phase, pos[axis]] = row
        copies = []
        for d in (4, 3, 5, 2, 6, 1, 7):
            copies.append(
                remote(
                    slots.at[pos[axis]], slots.at[pos[axis]],
                    sendr.at[phase, d - 1], recvr.at[phase, d - 1],
                    {axis: lax.rem(pos[axis] + d, RING)},
                )
            )
        for copy in copies:
            copy.start()
        if phase == 0:
            def terms(x, carry):
                for k in range(BLOCKS):
                    r = TOP + 8 * k
                    rows, own = pl.ds(r, 8), pl.ds(8 * k, 8)
                    p = fp[x + 1, rows]
                    pe = place(x, k, zmix[1])
                    gu = (
                        -0.5 * (fp[x + 2, rows] - p),
                        -0.5 * (fp[x + 1, pl.ds(r + 1, 8)] - p),
                        -0.5 * (above(p, pe) - p),
                    )
                    gd = (
                        -0.5 * (p - fp[x, rows]),
                        -0.5 * (p - fp[x + 1, pl.ds(r - 1, 8)]),
                        -0.5 * (p - below(p, pe)),
                    )
                    u2 = fu2[x + 1, rows]
                    bases[0, x, own] = (
                        (gd[0] * fu0[x, rows] + gu[0] * fu0[x + 1, rows])
                        + (gd[1] * fu1[x + 1, pl.ds(r - 1, 8)] + gu[1] * fu1[x + 1, rows])
                        + (gd[2] * below(u2, place(x, k, zmix[2])) + gu[2] * u2)
                    )
                    for i, field in enumerate((fv0, fv1, fv2)):
                        v, up, down = around(x, k, i, field)
                        total = None
                        for dim in range(3):
                            upper, lower = up[dim] - v, v - down[dim]
                            grads[i, dim, x, own] = upper
                            term = gd[dim] * lower + gu[dim] * upper
                            total = term if total is None else total + term
                        bases[1 + i, x, own] = total
                return carry

            lax.fori_loop(0, NXL, terms, 0)
        for copy in copies:
            copy.wait()
        parts = [sums[phase, i] for i in range(RING)]
        errs = []
        while len(parts) > 1:
            pairs = [two_sum(parts[i], parts[i + 1]) for i in range(0, len(parts), 2)]
            parts = [s for s, _ in pairs]
            errs.append(sum_tree([e for _, e in pairs]))
        total, err = parts[0], sum_tree(errs)
        row = jnp.where(low_half, total, total + roll(err, 64, 1))

    spread = jnp.broadcast_to(row, (8, NZL))
    col_hi = jnp.sum(jnp.where(lane == sub, spread, 0.0), axis=1, keepdims=True)
    col_lo = jnp.sum(jnp.where(lane == sub + 64, spread, 0.0), axis=1, keepdims=True)
    col_hi = jnp.broadcast_to(col_hi, (8, NZL))
    col_lo = jnp.broadcast_to(col_lo, (8, NZL))
    order = ROW_OF
    sums_hi_lo = [(col_hi[order[i] : order[i] + 1], col_lo[order[i] : order[i] + 1]) for i in range(8)]
    y = [jnp.broadcast_to(value, (8, NZL)) for value in galerkin(sums_hi_lo)]

    def finish(x, carry):
        for k in range(BLOCKS):
            rows, own = pl.ds(TOP + 8 * k, 8), pl.ds(8 * k, 8)
            for dim, field in enumerate((fu0, fu1, fu2)):
                grad = y[0] * grads[0, dim, x, own] + y[1] * grads[1, dim, x, own] + y[2] * grads[2, dim, x, own]
                out_u[dim, x, own] = field[x + 1, rows] + grad
            out_c[x, own] = bases[0, x, own] + (
                y[0] * bases[1, x, own] + y[1] * bases[2, x, own] + y[2] * bases[3, x, own]
            )
        return carry

    lax.fori_loop(0, NXL, finish, 0, unroll=4)
    stores = [
        pltpu.make_async_copy(out_u, ustar_hbm, store_sem.at[0]),
        pltpu.make_async_copy(out_c, coef_hbm, store_sem.at[1]),
    ]
    for store in stores:
        store.start()
    for copy in round1:
        copy.wait_send()
    for store in stores:
        store.wait()


def roll_rows(x, width, keep):
    if width == 4:
        return roll(x, 4, 0)
    return jnp.where(keep, roll(x, 8 - width, 0), roll(x, width, 0))


def sum_tree(values):
    total = values[0]
    for value in values[1:]:
        total = total + value
    return total


def row_order():
    level = [{i: set(range(8))} for i in range(8)]
    names = [[i] * 8 for i in range(8)]
    for width in (4, 2, 1):
        n = len(names) // 2
        names = [
            [names[i][r] if (r // width) % 2 == 0 else names[i + n][r] for r in range(8)] for i in range(n)
        ]
    return [names[0].index(i) for i in range(8)]


ROW_OF = row_order()


def on_device(phase_mask, pressure, velocity_cot):
    field = pltpu.VMEM((NXL + 2, 48, NZL), F32)
    block = pltpu.VMEM((NXL, NYL, NZL), F32)
    dma = pltpu.SemaphoreType.DMA
    anywhere = pl.BlockSpec(memory_space=pl.ANY)
    return pl.pallas_call(
        body,
        out_shape=(
            jax.ShapeDtypeStruct((3, NXL, NYL, NZL), F32),
            jax.ShapeDtypeStruct((NXL, NYL, NZL), F32),
        ),
        in_specs=[anywhere] * 3,
        out_specs=(anywhere, anywhere),
        scratch_shapes=[
            pltpu.VMEM((NXL, NYL, NZL), jnp.int32),
            field, field, field, field, field, field, field, field,
            pltpu.VMEM((NXL + 1, NYL, NZL), F32),
            block, block, block, block, block, block, block,
            pltpu.VMEM((3, 3, NXL, NYL, NZL), F32),
            pltpu.VMEM((4, NXL, NYL, NZL), F32),
            pltpu.VMEM((3, NXL, NZL), F32),
            pltpu.VMEM((2, NXL, NZL), F32),
            pltpu.VMEM((3, NXL, NZL), F32),
            pltpu.VMEM((2, NXL, NZL), F32),
            pltpu.VMEM((NXL, NZL), F32),
            pltpu.VMEM((NXL, NZL), F32),
            pltpu.VMEM((3, NXL, NZL), F32),
            pltpu.VMEM((3, NXL, NZL), F32),
            pltpu.VMEM((3, 8, NZL), F32),
            pltpu.VMEM((3, 8, NZL), F32),
            pltpu.VMEM((3, 8, NZL), F32),
            pltpu.VMEM((3, 8, NZL), F32),
            pltpu.VMEM((3, 8, NZL), F32),
            pltpu.VMEM((3, 8, NZL), F32),
            pltpu.VMEM((3, 8, NZL), F32),
            pltpu.VMEM((3, 8, NZL), F32),
            pltpu.VMEM((3, RING, 1, NZL), F32),
            pltpu.VMEM((3, NXL, NYL, NZL), F32),
            block,
            dma((5,)), dma((2,)),
            dma((9,)), dma((9,)), dma((3, 6)), dma((3, 6)), dma((3, 7)), dma((3, 7)),
        ],
        compiler_params=pltpu.CompilerParams(collective_id=0, has_side_effects=True),
        name="projection_adjoint",
    )(phase_mask, pressure, velocity_cot)


def solution(mesh):
    in_specs = (P("gx", "gy", "gz"), P("gx", "gy", "gz"), P(None, "gx", "gy", "gz"))
    out_specs = (P(None, "gx", "gy", "gz"), P("gx", "gy", "gz"))
    return jax.shard_map(
        on_device, mesh=mesh, in_specs=in_specs, out_specs=out_specs, check_vma=False
    )
```

time: 681 us -> 47.8 us (0.07)
  blocking collectives: 499 us -> 0 us
  starting transfers between devices: 88.3 us -> 0 us
  waiting for transfers between devices: 45.6 us -> 0 us
  Pallas kernels: 0 us -> 44.2 us
  other arithmetic: 26 us -> 0 us
  local copies, waits for them, and re-layouts: 11.8 us -> 2.81 us
  between operations: 7.69 us -> 0.65 us
    psum x5 -> x0, blocking collectives: 499 us -> none  [the longest x3 299 us: norm_sum(): return lax.psum(jnp.sum(resid * precd), ('gx', 'gy', 'gz'))]
    ppermute x30 -> x0, starting transfers between devices: 88.3 us -> none  [the longest x15 60.3 us: extended(): lax.ppermute(tail, axis, [(i, (i + 1) % count) for i in range(ends)])]
    ppermute x30 -> x0, waiting for transfers between devices: 45.6 us -> none  [the longest x15 33.7 us: extended(): lax.ppermute(head, axis, [((i + 1) % count, i) for i in range(ends)])]
    pallas_call x0 -> x1, Pallas kernels: none -> 44.2 us  [on_device(): pl.pallas_call(body, out_shape=(jax.ShapeDtypeStruct((3, NXL, NYL, NZL),...]
    reduce_sum x5 -> x0, other arithmetic: 7.91 us -> none  [the longest x2 4.16 us: norm_sum(): return lax.psum(jnp.sum(resid * precd), ('gx', 'gy', 'gz'))]
  transfers between devices with their start and end apart: 30 -> 0, of which waited for: 19 -> 0; matrix products, arithmetic and copies ran while one was open for 1% -> 0% of each run, Pallas kernels for 0% -> 0%
where the time goes in v1:
time: 47.8 us; the launch traced here: 47.6 us
  Pallas kernels  44.2 us (92%)
  local copies, waits for them, and re-layouts  2.81 us (6%)
  between operations  0.65 us (1%)
    pallas_call x1, Pallas kernels, on_device(): pl.pallas_call(body, out_shape=(jax.ShapeDtypeStruct((3, NXL, NYL, NZL),...  44.2 us
    unnamed x4, local copies, waits for them, and re-layouts  2.81 us

profile of v1, /device:TPU:1, one launch (start us, length us, event | category | flops | bytes accessed | tf_op | source)
XLA Modules:
  0.0 47.6 jit_solution(1455408176084637704)
XLA Ops:
  0.6 44.2 %projection_adjoint.1 = (f32[3,16,32,128]{3,2,1,0:T(8,128)}, f32[16,32,128]{2,1,0:T(8,128)}) custom-call(s32[16,32,128]{2,1,0:T(8,128)} %mask_hbm.1, f32[16,32,128]{2,1,0:T(8,128)} %press_hbm.1, f32[3,16,32,128]{3,2,1,0:T(8,128)} %vel_hbm.1), custom_call_target="tpu_custom_call" | custom-call | tf_op jit(solution)/shard_map/projection_adjoint/pallas_call | solution.py:479
  44.8 0.0 copy-start
  44.8 2.1 %copy.7 = f32[3,16,32,128]{3,2,1,0:T(8,128)} copy(f32[3,16,32,128]{3,2,1,0:T(8,128)} %get-tuple-element.4) | data formatting | bytes 1572864
  46.9 0.0 copy-done
  46.9 0.7 %copy.8 = f32[16,32,128]{2,1,0:T(8,128)} copy(f32[16,32,128]{2,1,0:T(8,128)S(1)} %copy-done) | data formatting | bytes 524288
Async XLA Ops:
  44.8 2.1 %copy-start = (f32[16,32,128]{2,1,0:T(8,128)S(1)}, f32[16,32,128]{2,1,0:T(8,128)}, u32[]{:S(2)}) copy-start(f32[16,32,128]{2,1,0:T(8,128)} %get-tuple-element.5) | copy-start | bytes 786436

commit v2 on v1

--- a/solution.py
+++ b/solution.py
@@ -14,6 +14,7 @@
 LAST = TOP + NYL - 1
 BLOCKS = NYL // 8
 F32 = jnp.float32
+PHASES = (("gy",), ("gx", "gz"))
 
 
 def two_sum(a, b):
@@ -77,15 +78,15 @@
 
 
 def body(
-    mask_hbm, press_hbm, vel_hbm, ustar_hbm, coef_hbm,
+    mask_hbm, press_hbm, vel_hbm, out_u, out_c,
     mask, fc, fp, fu0, fu1, fu2, fv0, fv1, fv2,
     wx, wyu, wyd, wzu, wzd, minv, rhs, img,
     grads, bases,
-    yup, ydn, yup_in, ydn_in, vyup, vydn, vyup_in, vydn_in,
-    zup, zin_lo, zin_hi, zmix, vz, vz_lo, vz_hi, vmix,
-    sums, out_u, out_c,
-    load_sem, store_sem,
-    send1, recv1, sendv, recvv, sendr, recvr,
+    yup, ydn, yup_in, ydn_in, pyup, pydn, pyup_in, pydn_in, vyup, vydn, vyup_in, vydn_in,
+    zup, zin_lo, zin_hi, pz, pz_lo, pz_hi, zmix, vz, vz_lo, vz_hi, vmix,
+    sums,
+    load_sem,
+    send1, recv1, sendv, recvv, sendr, recvr, ready,
 ):
     pos = {axis: lax.axis_index(axis) for axis in AXES}
     fwd = {axis: lax.rem(pos[axis] + 1, RING) for axis in AXES}
@@ -136,18 +137,18 @@
             pp = pick(x, k, fp[x + 1, rows], pp)
             pu = pick(x, k, fu2[x + 1, rows], pu)
             if k == 0:
-                ydn[0, pl.ds(x, 1)] = c[0:1]
-                ydn[1, pl.ds(x, 1)] = fp[x + 1, pl.ds(TOP, 1)]
+                ydn[pl.ds(x, 1)] = c[0:1]
+                pydn[pl.ds(x, 1)] = fp[x + 1, pl.ds(TOP, 1)]
             if k == BLOCKS - 1:
                 yup[0, pl.ds(x, 1)] = c[7:8]
-                yup[1, pl.ds(x, 1)] = fp[x + 1, pl.ds(LAST, 1)]
-                yup[2, pl.ds(x, 1)] = fu1[x + 1, pl.ds(LAST, 1)]
+                pyup[pl.ds(x, 1)] = fp[x + 1, pl.ds(LAST, 1)]
+                yup[1, pl.ds(x, 1)] = fu1[x + 1, pl.ds(LAST, 1)]
         return pc, pp, pu
 
     pc, pp, pu = lax.fori_loop(0, NXL, prepare, (zero, zero, zero), unroll=4)
     zup[0] = pc
-    zup[1] = pp
-    zup[2] = pu
+    zup[1] = pu
+    pz[...] = pp
 
     pl.semaphore_wait(barrier, 6)
 
@@ -155,18 +156,25 @@
     round1 = [
         remote(fc.at[NXL, inner], fc.at[0, inner], send1.at[0], recv1.at[0], {"gx": fwd["gx"]}),
         remote(fc.at[1, inner], fc.at[NXL + 1, inner], send1.at[1], recv1.at[1], {"gx": bwd["gx"]}),
-        remote(fu0.at[NXL, inner], fu0.at[0, inner], send1.at[2], recv1.at[2], {"gx": fwd["gx"]}),
-        remote(fp.at[NXL, inner], fp.at[0, inner], send1.at[3], recv1.at[3], {"gx": fwd["gx"]}),
-        remote(fp.at[1, inner], fp.at[NXL + 1, inner], send1.at[4], recv1.at[4], {"gx": bwd["gx"]}),
-        remote(yup, yup_in, send1.at[5], recv1.at[5], {"gy": fwd["gy"]}),
-        remote(ydn, ydn_in, send1.at[6], recv1.at[6], {"gy": bwd["gy"]}),
-        remote(zup, zin_lo, send1.at[7], recv1.at[7], {"gz": fwd["gz"]}),
-        remote(zup, zin_hi, send1.at[8], recv1.at[8], {"gz": bwd["gz"]}),
+        remote(yup, yup_in, send1.at[2], recv1.at[2], {"gy": fwd["gy"]}),
+        remote(ydn, ydn_in, send1.at[3], recv1.at[3], {"gy": bwd["gy"]}),
+        remote(zup, zin_lo, send1.at[4], recv1.at[4], {"gz": fwd["gz"]}),
+        remote(zup, zin_hi, send1.at[5], recv1.at[5], {"gz": bwd["gz"]}),
+        remote(fu0.at[NXL, inner], fu0.at[0, inner], send1.at[6], recv1.at[6], {"gx": fwd["gx"]}),
     ]
     for copy in round1:
         copy.start()
+    later = [
+        remote(fp.at[NXL, inner], fp.at[0, inner], send1.at[7], recv1.at[7], {"gx": fwd["gx"]}),
+        remote(fp.at[1, inner], fp.at[NXL + 1, inner], send1.at[8], recv1.at[8], {"gx": bwd["gx"]}),
+        remote(pyup, pyup_in, send1.at[9], recv1.at[9], {"gy": fwd["gy"]}),
+        remote(pydn, pydn_in, send1.at[10], recv1.at[10], {"gy": bwd["gy"]}),
+        remote(pz, pz_lo, send1.at[11], recv1.at[11], {"gz": fwd["gz"]}),
+        remote(pz, pz_hi, send1.at[12], recv1.at[12], {"gz": bwd["gz"]}),
+    ]
     for copy in round1:
         copy.wait_recv()
+    sent = round1 + later
 
     low = {axis: pos[axis] == 0 for axis in AXES}
     high = {axis: pos[axis] == RING - 1 for axis in AXES}
@@ -187,24 +195,22 @@
         hi = jnp.where(high["gz"], 0.0, hi)
         return jnp.where(even, roll(hi, NZL - 1, 1), roll(lo, 1, 1))
 
-    clear_x((fc, fp, fu0), (fc, fp))
-    for i in range(3):
-        zmix[i] = mix(zin_lo[i], zin_hi[i])
+    clear_x((fc, fu0), (fc,))
+    zmix[0] = mix(zin_lo[0], zin_hi[0])
+    zmix[2] = mix(zin_lo[1], zin_hi[1])
     for x in range(NXL):
         row = pl.ds(x, 1)
         fc[x + 1, pl.ds(TOP - 1, 1)] = jnp.where(low["gy"], 0.0, yup_in[0, row])
-        fp[x + 1, pl.ds(TOP - 1, 1)] = jnp.where(low["gy"], 0.0, yup_in[1, row])
-        fu1[x + 1, pl.ds(TOP - 1, 1)] = jnp.where(low["gy"], 0.0, yup_in[2, row])
-        fc[x + 1, pl.ds(LAST + 1, 1)] = jnp.where(high["gy"], 0.0, ydn_in[0, row])
-        fp[x + 1, pl.ds(LAST + 1, 1)] = jnp.where(high["gy"], 0.0, ydn_in[1, row])
+        fu1[x + 1, pl.ds(TOP - 1, 1)] = jnp.where(low["gy"], 0.0, yup_in[1, row])
+        fc[x + 1, pl.ds(LAST + 1, 1)] = jnp.where(high["gy"], 0.0, ydn_in[row])
 
     wx[0] = 0.5 * (fc[0, inner] + fc[1, inner])
 
-    def faces(x, k, value):
+    def faces(i, x, k, value):
         if k == 0:
-            vydn[pl.ds(x, 1)] = value[0:1]
+            vydn[i, pl.ds(x, 1)] = value[0:1]
         if k == BLOCKS - 1:
-            vyup[pl.ds(x, 1)] = value[7:8]
+            vyup[i, pl.ds(x, 1)] = value[7:8]
 
     def start(x, carry):
         packed, g0 = carry
@@ -236,7 +242,7 @@
             rhs[x, own] = r0
             fv0[x + 1, rows] = v
             packed = pick(x, k, v, packed)
-            faces(x, k, v)
+            faces(0, x, k, v)
             g0 = g0 + v * r0
         return packed, g0
 
@@ -247,15 +253,19 @@
         copies = [
             remote(field.at[NXL, inner], field.at[0, inner], sendv.at[i, 0], recvv.at[i, 0], {"gx": fwd["gx"]}),
             remote(field.at[1, inner], field.at[NXL + 1, inner], sendv.at[i, 1], recvv.at[i, 1], {"gx": bwd["gx"]}),
-            remote(vyup, vyup_in.at[i], sendv.at[i, 2], recvv.at[i, 2], {"gy": fwd["gy"]}),
-            remote(vydn, vydn_in.at[i], sendv.at[i, 3], recvv.at[i, 3], {"gy": bwd["gy"]}),
+            remote(vyup.at[i], vyup_in.at[i], sendv.at[i, 2], recvv.at[i, 2], {"gy": fwd["gy"]}),
+            remote(vydn.at[i], vydn_in.at[i], sendv.at[i, 3], recvv.at[i, 3], {"gy": bwd["gy"]}),
             remote(vz.at[i], vz_lo.at[i], sendv.at[i, 4], recvv.at[i, 4], {"gz": fwd["gz"]}),
             remote(vz.at[i], vz_hi.at[i], sendv.at[i, 5], recvv.at[i, 5], {"gz": bwd["gz"]}),
         ]
         for copy in copies:
             copy.start()
+        if i == 0:
+            for copy in later:
+                copy.start()
         for copy in copies:
-            copy.wait()
+            copy.wait_recv()
+        sent.extend(copies)
         clear_x((field,), (field,))
         vmix[i] = mix(vz_lo[i], vz_hi[i])
         for x in range(NXL):
@@ -295,13 +305,17 @@
             img[x, own] = q
             fv1[x + 1, pl.ds(TOP + 8 * k, 8)] = w
             packed = pick(x, k, w, packed)
-            faces(x, k, w)
+            faces(1, x, k, w)
             h00 = h00 + v * q
             h01 = h01 + w * q
         return packed, h00, h01
 
     packed, h00, h01 = lax.fori_loop(0, NXL, step0, (zero, zero, zero), unroll=4)
     exchange(1, fv1, packed)
+    for d in range(1, RING):
+        pl.semaphore_signal(
+            ready, inc=1, device_id={"gz": lax.rem(pos["gz"] + d, RING)}, device_id_type=MESH
+        )
 
     def step1(x, carry):
         packed, h02, h11, h12, g2 = carry
@@ -311,7 +325,7 @@
             w = minv[x, own] * q - v
             fv2[x + 1, pl.ds(TOP + 8 * k, 8)] = w
             packed = pick(x, k, w, packed)
-            faces(x, k, w)
+            faces(2, x, k, w)
             h02 = h02 + w * img[x, own]
             h11 = h11 + v * q
             h12 = h12 + w * q
@@ -351,21 +365,34 @@
 
     low_half = lax.broadcasted_iota(jnp.int32, (1, NZL), 1) < 64
 
-    for phase, axis in enumerate(("gy", "gx", "gz")):
-        slots = sums.at[phase]
-        sums[phase, pos[axis]] = row
-        copies = []
-        for d in (4, 3, 5, 2, 6, 1, 7):
-            copies.append(
-                remote(
-                    slots.at[pos[axis]], slots.at[pos[axis]],
-                    sendr.at[phase, d - 1], recvr.at[phase, d - 1],
-                    {axis: lax.rem(pos[axis] + d, RING)},
-                )
-            )
-        for copy in copies:
-            copy.start()
+    slot0 = 0
+    drains = []
+    for phase, axes in enumerate(PHASES):
+        count = RING ** len(axes)
+        mine = 0
+        for axis in axes:
+            mine = mine * RING + pos[axis]
+        slots = sums.at[pl.ds(slot0, count)]
+        slots[mine] = row
+        if len(axes) > 1:
+            pl.semaphore_wait(ready, RING - 1)
+        offsets = [()]
+        for axis in axes:
+            offsets = [o + (d,) for o in offsets for d in range(RING)]
+        offsets = sorted(offsets[1:], key=lambda o: -sum(min(d, RING - d) for d in o))
+        for o in offsets:
+            device = {axis: lax.rem(pos[axis] + d, RING) for axis, d in zip(axes, o) if d}
+            remote(slots.at[mine], slots.at[mine], sendr.at[phase], recvr.at[phase], device).start()
         if phase == 0:
+            for copy in later:
+                copy.wait_recv()
+            clear_x((fp,), (fp,))
+            zmix[1] = mix(pz_lo[...], pz_hi[...])
+            for x in range(NXL):
+                lrow = pl.ds(x, 1)
+                fp[x + 1, pl.ds(TOP - 1, 1)] = jnp.where(low["gy"], 0.0, pyup_in[lrow])
+                fp[x + 1, pl.ds(LAST + 1, 1)] = jnp.where(high["gy"], 0.0, pydn_in[lrow])
+
             def terms(x, carry):
                 for k in range(BLOCKS):
                     r = TOP + 8 * k
@@ -400,9 +427,10 @@
                 return carry
 
             lax.fori_loop(0, NXL, terms, 0)
-        for copy in copies:
-            copy.wait()
-        parts = [sums[phase, i] for i in range(RING)]
+        others = sums.at[pl.ds(slot0, count - 1)]
+        pltpu.make_async_copy(others, others, recvr.at[phase]).wait()
+        drains.append(pltpu.make_async_copy(others, others, sendr.at[phase]))
+        parts = [sums[slot0 + i] for i in range(count)]
         errs = []
         while len(parts) > 1:
             pairs = [two_sum(parts[i], parts[i + 1]) for i in range(0, len(parts), 2)]
@@ -410,6 +438,7 @@
             errs.append(sum_tree([e for _, e in pairs]))
         total, err = parts[0], sum_tree(errs)
         row = jnp.where(low_half, total, total + roll(err, 64, 1))
+        slot0 += count
 
     spread = jnp.broadcast_to(row, (8, NZL))
     col_hi = jnp.sum(jnp.where(lane == sub, spread, 0.0), axis=1, keepdims=True)
@@ -432,16 +461,10 @@
         return carry
 
     lax.fori_loop(0, NXL, finish, 0, unroll=4)
-    stores = [
-        pltpu.make_async_copy(out_u, ustar_hbm, store_sem.at[0]),
-        pltpu.make_async_copy(out_c, coef_hbm, store_sem.at[1]),
-    ]
-    for store in stores:
-        store.start()
-    for copy in round1:
+    for drain in drains:
+        drain.wait()
+    for copy in sent:
         copy.wait_send()
-    for store in stores:
-        store.wait()
 
 
 def roll_rows(x, width, keep):
@@ -471,51 +494,72 @@
 ROW_OF = row_order()
 
 
+def save(ustar, coef, ustar_hbm, coef_hbm, sem):
+    stores = [
+        pltpu.make_async_copy(ustar, ustar_hbm, sem.at[0]),
+        pltpu.make_async_copy(coef, coef_hbm, sem.at[1]),
+    ]
+    for store in stores:
+        store.start()
+    for store in stores:
+        store.wait()
+
+
 def on_device(phase_mask, pressure, velocity_cot):
     field = pltpu.VMEM((NXL + 2, 48, NZL), F32)
     block = pltpu.VMEM((NXL, NYL, NZL), F32)
+    flat = pltpu.VMEM((NXL, NZL), F32)
+    flats = pltpu.VMEM((3, NXL, NZL), F32)
+    tile = pltpu.VMEM((8, NZL), F32)
+    tiles = pltpu.VMEM((3, 8, NZL), F32)
     dma = pltpu.SemaphoreType.DMA
-    anywhere = pl.BlockSpec(memory_space=pl.ANY)
-    return pl.pallas_call(
+    in_hbm = pl.BlockSpec(memory_space=pltpu.HBM)
+    in_vmem = pl.BlockSpec(memory_space=pltpu.VMEM)
+    out_shape = (
+        jax.ShapeDtypeStruct((3, NXL, NYL, NZL), F32),
+        jax.ShapeDtypeStruct((NXL, NYL, NZL), F32),
+    )
+    inputs = [
+        pltpu.with_memory_space_constraint(a, pltpu.HBM) for a in (phase_mask, pressure, velocity_cot)
+    ]
+    outs = pl.pallas_call(
         body,
-        out_shape=(
-            jax.ShapeDtypeStruct((3, NXL, NYL, NZL), F32),
-            jax.ShapeDtypeStruct((NXL, NYL, NZL), F32),
-        ),
-        in_specs=[anywhere] * 3,
-        out_specs=(anywhere, anywhere),
+        out_shape=out_shape,
+        in_specs=[in_hbm] * 3,
+        out_specs=(in_vmem, in_vmem),
         scratch_shapes=[
             pltpu.VMEM((NXL, NYL, NZL), jnp.int32),
-            field, field, field, field, field, field, field, field,
+            *[field] * 8,
             pltpu.VMEM((NXL + 1, NYL, NZL), F32),
-            block, block, block, block, block, block, block,
+            *[block] * 7,
             pltpu.VMEM((3, 3, NXL, NYL, NZL), F32),
             pltpu.VMEM((4, NXL, NYL, NZL), F32),
-            pltpu.VMEM((3, NXL, NZL), F32),
-            pltpu.VMEM((2, NXL, NZL), F32),
-            pltpu.VMEM((3, NXL, NZL), F32),
-            pltpu.VMEM((2, NXL, NZL), F32),
-            pltpu.VMEM((NXL, NZL), F32),
-            pltpu.VMEM((NXL, NZL), F32),
-            pltpu.VMEM((3, NXL, NZL), F32),
-            pltpu.VMEM((3, NXL, NZL), F32),
-            pltpu.VMEM((3, 8, NZL), F32),
-            pltpu.VMEM((3, 8, NZL), F32),
-            pltpu.VMEM((3, 8, NZL), F32),
-            pltpu.VMEM((3, 8, NZL), F32),
-            pltpu.VMEM((3, 8, NZL), F32),
-            pltpu.VMEM((3, 8, NZL), F32),
-            pltpu.VMEM((3, 8, NZL), F32),
-            pltpu.VMEM((3, 8, NZL), F32),
-            pltpu.VMEM((3, RING, 1, NZL), F32),
-            pltpu.VMEM((3, NXL, NYL, NZL), F32),
-            block,
-            dma((5,)), dma((2,)),
-            dma((9,)), dma((9,)), dma((3, 6)), dma((3, 6)), dma((3, 7)), dma((3, 7)),
+            pltpu.VMEM((2, NXL, NZL), F32), flat, pltpu.VMEM((2, NXL, NZL), F32), flat,
+            *[flat] * 4,
+            *[flats] * 4,
+            *[pltpu.VMEM((2, 8, NZL), F32)] * 3,
+            *[tile] * 3,
+            *[tiles] * 5,
+            pltpu.VMEM((sum(RING ** len(axes) for axes in PHASES), 1, NZL), F32),
+            dma((5,)),
+            dma((13,)), dma((13,)), dma((3, 6)), dma((3, 6)),
+            dma((len(PHASES),)), dma((len(PHASES),)),
+            pltpu.SemaphoreType.REGULAR,
         ],
-        compiler_params=pltpu.CompilerParams(collective_id=0, has_side_effects=True),
+        compiler_params=pltpu.CompilerParams(
+            collective_id=0, has_side_effects=True, vmem_limit_bytes=24 * 1024 * 1024
+        ),
         name="projection_adjoint",
-    )(phase_mask, pressure, velocity_cot)
+    )(*inputs)
+    return pl.pallas_call(
+        save,
+        out_shape=out_shape,
+        in_specs=[in_vmem] * 2,
+        out_specs=(in_hbm, in_hbm),
+        scratch_shapes=[dma((2,))],
+        compiler_params=pltpu.CompilerParams(vmem_limit_bytes=4 * 1024 * 1024),
+        name="save",
+    )(*outs)
 
 
 def solution(mesh):

time: 47.8 us -> 43.3 us (0.906)
  local copies, waits for them, and re-layouts: 2.81 us -> 0 us
  Pallas kernels: 44.2 us -> 42.5 us
    unnamed x4 -> x0, local copies, waits for them, and re-layouts: 2.81 us -> none
    pallas_call x1 -> x2, Pallas kernels: 44.2 us -> 42.5 us  [the longest x1 41.5 us: on_device(): pl.pallas_call(body, out_shape=out_shape, in_specs=[in_hbm] * 3, out_spec...]
where the time goes in v2:
time: 43.3 us; the launch traced here: 43.1 us
  Pallas kernels  42.5 us (98%)
  between operations  0.64 us (1%)
    pallas_call x1, Pallas kernels, on_device(): pl.pallas_call(body, out_shape=out_shape, in_specs=[in_hbm] * 3, out_spec...  41.5 us
    pallas_call x1, Pallas kernels, on_device(): pl.pallas_call(save, out_shape=out_shape, in_specs=[in_vmem] * 2, out_spe...  0.98 us

profile of v2, /device:TPU:1, one launch (start us, length us, event | category | flops | bytes accessed | tf_op | source)
XLA Modules:
  0.0 43.1 jit_solution(6047344089966029795)
XLA Ops:
  0.6 41.5 %projection_adjoint.1 = (f32[3,16,32,128]{3,2,1,0:T(8,128)S(1)}, f32[16,32,128]{2,1,0:T(8,128)S(1)}) custom-call(s32[16,32,128]{2,1,0:T(8,128)} %mask_hbm.1, f32[16,32,128]{2,1,0:T(8,128)} %press_hbm.1, f32[3,16,32,128]{3,2,1,0:T(8,128)} %vel_hbm.1), custom_call_target="tpu_custom_call" | custom-call | tf_op jit(solution)/shard_map/projection_adjoint/pallas_call | solution.py:525
  42.1 1.0 %save.1 = (f32[3,16,32,128]{3,2,1,0:T(8,128)}, f32[16,32,128]{2,1,0:T(8,128)}) custom-call(f32[3,16,32,128]{3,2,1,0:T(8,128)S(1)} %get-tuple-element.4.ustar, f32[16,32,128]{2,1,0:T(8,128)S(1)} %get-tuple-element.5.coef), custom_call_target="tpu_custom_call" | custom-call | tf_op jit(solution)/shard_map/save/pallas_call | solution.py:554

commit v3 on v2

--- a/solution.py
+++ b/solution.py
@@ -80,13 +80,13 @@
 def body(
     mask_hbm, press_hbm, vel_hbm, out_u, out_c,
     mask, fc, fp, fu0, fu1, fu2, fv0, fv1, fv2,
-    wx, wyu, wyd, wzu, wzd, minv, rhs, img,
+    wx, wyu, wyd, wzu, wzd, wzb, wyb, minv, rhs, img, part,
     grads, bases,
-    yup, ydn, yup_in, ydn_in, pyup, pydn, pyup_in, pydn_in, vyup, vydn, vyup_in, vydn_in,
+    yup, ydn, yup_in, ydn_in, pyup, pydn, pyup_in, pydn_in, vyup, vydn, vy_in, vx_in,
     zup, zin_lo, zin_hi, pz, pz_lo, pz_hi, zmix, vz, vz_lo, vz_hi, vmix,
     sums,
     load_sem,
-    send1, recv1, sendv, recvv, sendr, recvr, ready,
+    send1, recv1, sendv, recvv, sendr, recvr, ready, token,
 ):
     pos = {axis: lax.axis_index(axis) for axis in AXES}
     fwd = {axis: lax.rem(pos[axis] + 1, RING) for axis in AXES}
@@ -97,6 +97,42 @@
     first = lane == 0
     final = lane == NZL - 1
 
+    low = {axis: pos[axis] == 0 for axis in AXES}
+    high = {axis: pos[axis] == RING - 1 for axis in AXES}
+
+    class Shift:
+        def __init__(self, src, dst, send, recv, axis, up):
+            other = fwd[axis] if up else bwd[axis]
+            self.copy = remote(src, dst, send, recv, {axis: other})
+            self.sends = jnp.logical_not(high[axis] if up else low[axis])
+            self.receives = jnp.logical_not(low[axis] if up else high[axis])
+
+        def start(self):
+            pl.when(self.sends)(lambda: self.copy.start())
+
+        def wait_recv(self):
+            pl.when(self.receives)(lambda: self.copy.wait_recv())
+
+        def wait_send(self):
+            pl.when(self.sends)(lambda: self.copy.wait_send())
+
+    def tell(stage):
+        for a, axis in enumerate(AXES):
+            for end, other in ((high[axis], fwd[axis]), (low[axis], bwd[axis])):
+
+                @pl.when(end)
+                def _(a=a, axis=axis, other=other):
+                    pl.semaphore_signal(
+                        token.at[stage, a], inc=1, device_id={axis: other}, device_id_type=MESH
+                    )
+
+    def heard(stage):
+        for a, axis in enumerate(AXES):
+
+            @pl.when(jnp.logical_or(high[axis], low[axis]))
+            def _(a=a):
+                pl.semaphore_wait(token.at[stage, a], 1)
+
     cells = (pl.ds(1, NXL), pl.ds(TOP, NYL))
     loads = [pltpu.make_async_copy(mask_hbm, mask, load_sem.at[0])]
     for i, field in enumerate((fu0, fu1, fu2)):
@@ -105,6 +141,20 @@
     for load in loads:
         load.start()
 
+    inner = pl.ds(TOP, NYL)
+    plane = jnp.zeros((NYL, NZL), F32)
+    line = jnp.zeros((1, NZL), F32)
+    zero = jnp.zeros((8, NZL), F32)
+    for field in (fc, fp, fu0, fv0, fv1, fv2):
+        field[0, inner] = plane
+        field[NXL + 1, inner] = plane
+    for x in range(1, NXL + 1):
+        for field in (fv0, fv1, fv2):
+            field[x, pl.ds(TOP - 1, 1)] = line
+            field[x, pl.ds(LAST + 1, 1)] = line
+    for buffer in (yup_in, ydn_in, pyup_in, pydn_in, vy_in, vx_in, zin_lo, zin_hi, pz_lo, pz_hi, vz_lo, vz_hi):
+        buffer[...] = jnp.zeros(buffer.shape, F32)
+
     barrier = pltpu.get_barrier_semaphore()
     for axis in AXES:
         for other in (fwd[axis], bwd[axis]):
@@ -123,8 +173,6 @@
 
     def below(value, edge):
         return jnp.where(first, edge, roll(value, 1, 1))
-
-    zero = jnp.zeros((8, NZL), F32)
 
     def prepare(x, carry):
         pc, pp, pu = carry
@@ -152,57 +200,40 @@
 
     pl.semaphore_wait(barrier, 6)
 
-    inner = pl.ds(TOP, NYL)
     round1 = [
-        remote(fc.at[NXL, inner], fc.at[0, inner], send1.at[0], recv1.at[0], {"gx": fwd["gx"]}),
-        remote(fc.at[1, inner], fc.at[NXL + 1, inner], send1.at[1], recv1.at[1], {"gx": bwd["gx"]}),
-        remote(yup, yup_in, send1.at[2], recv1.at[2], {"gy": fwd["gy"]}),
-        remote(ydn, ydn_in, send1.at[3], recv1.at[3], {"gy": bwd["gy"]}),
-        remote(zup, zin_lo, send1.at[4], recv1.at[4], {"gz": fwd["gz"]}),
-        remote(zup, zin_hi, send1.at[5], recv1.at[5], {"gz": bwd["gz"]}),
-        remote(fu0.at[NXL, inner], fu0.at[0, inner], send1.at[6], recv1.at[6], {"gx": fwd["gx"]}),
+        Shift(fc.at[NXL, inner], fc.at[0, inner], send1.at[0], recv1.at[0], "gx", True),
+        Shift(fc.at[1, inner], fc.at[NXL + 1, inner], send1.at[1], recv1.at[1], "gx", False),
+        Shift(yup, yup_in, send1.at[2], recv1.at[2], "gy", True),
+        Shift(ydn, ydn_in, send1.at[3], recv1.at[3], "gy", False),
+        Shift(zup, zin_lo, send1.at[4], recv1.at[4], "gz", True),
+        Shift(zup, zin_hi, send1.at[5], recv1.at[5], "gz", False),
+        Shift(fu0.at[NXL, inner], fu0.at[0, inner], send1.at[6], recv1.at[6], "gx", True),
     ]
     for copy in round1:
         copy.start()
+    tell(0)
     later = [
-        remote(fp.at[NXL, inner], fp.at[0, inner], send1.at[7], recv1.at[7], {"gx": fwd["gx"]}),
-        remote(fp.at[1, inner], fp.at[NXL + 1, inner], send1.at[8], recv1.at[8], {"gx": bwd["gx"]}),
-        remote(pyup, pyup_in, send1.at[9], recv1.at[9], {"gy": fwd["gy"]}),
-        remote(pydn, pydn_in, send1.at[10], recv1.at[10], {"gy": bwd["gy"]}),
-        remote(pz, pz_lo, send1.at[11], recv1.at[11], {"gz": fwd["gz"]}),
-        remote(pz, pz_hi, send1.at[12], recv1.at[12], {"gz": bwd["gz"]}),
+        Shift(fp.at[NXL, inner], fp.at[0, inner], send1.at[7], recv1.at[7], "gx", True),
+        Shift(fp.at[1, inner], fp.at[NXL + 1, inner], send1.at[8], recv1.at[8], "gx", False),
+        Shift(pyup, pyup_in, send1.at[9], recv1.at[9], "gy", True),
+        Shift(pydn, pydn_in, send1.at[10], recv1.at[10], "gy", False),
+        Shift(pz, pz_lo, send1.at[11], recv1.at[11], "gz", True),
+        Shift(pz, pz_hi, send1.at[12], recv1.at[12], "gz", False),
     ]
     for copy in round1:
         copy.wait_recv()
     sent = round1 + later
 
-    low = {axis: pos[axis] == 0 for axis in AXES}
-    high = {axis: pos[axis] == RING - 1 for axis in AXES}
-
-    def clear_x(fields_low, fields_high):
-        @pl.when(low["gx"])
-        def _():
-            for field in fields_low:
-                field[0, inner] = jnp.zeros((NYL, NZL), F32)
-
-        @pl.when(high["gx"])
-        def _():
-            for field in fields_high:
-                field[NXL + 1, inner] = jnp.zeros((NYL, NZL), F32)
-
     def mix(lo, hi):
-        lo = jnp.where(low["gz"], 0.0, lo)
-        hi = jnp.where(high["gz"], 0.0, hi)
         return jnp.where(even, roll(hi, NZL - 1, 1), roll(lo, 1, 1))
 
-    clear_x((fc, fu0), (fc,))
     zmix[0] = mix(zin_lo[0], zin_hi[0])
     zmix[2] = mix(zin_lo[1], zin_hi[1])
     for x in range(NXL):
         row = pl.ds(x, 1)
-        fc[x + 1, pl.ds(TOP - 1, 1)] = jnp.where(low["gy"], 0.0, yup_in[0, row])
-        fu1[x + 1, pl.ds(TOP - 1, 1)] = jnp.where(low["gy"], 0.0, yup_in[1, row])
-        fc[x + 1, pl.ds(LAST + 1, 1)] = jnp.where(high["gy"], 0.0, ydn_in[row])
+        fc[x + 1, pl.ds(TOP - 1, 1)] = yup_in[0, row]
+        fu1[x + 1, pl.ds(TOP - 1, 1)] = yup_in[1, row]
+        fc[x + 1, pl.ds(LAST + 1, 1)] = ydn_in[row]
 
     wx[0] = 0.5 * (fc[0, inner] + fc[1, inner])
 
@@ -213,7 +244,7 @@
             vyup[i, pl.ds(x, 1)] = value[7:8]
 
     def start(x, carry):
-        packed, g0 = carry
+        packed, pw, g0 = carry
         for k in range(BLOCKS):
             r = TOP + 8 * k
             rows, own = pl.ds(r, 8), pl.ds(8 * k, 8)
@@ -240,38 +271,79 @@
             wzd[x, own] = zd
             minv[x, own] = m
             rhs[x, own] = r0
+            zb = jnp.where(first, zd, jnp.where(final, zu, 0.0))
+            wzb[x, own] = zb
+            pw = pick(x, k, zb, pw)
+            if k == 0:
+                wyb[0, pl.ds(x, 1)] = yd[0:1]
+            if k == BLOCKS - 1:
+                wyb[1, pl.ds(x, 1)] = yu[7:8]
             fv0[x + 1, rows] = v
             packed = pick(x, k, v, packed)
             faces(0, x, k, v)
             g0 = g0 + v * r0
-        return packed, g0
-
-    packed, g0 = lax.fori_loop(0, NXL, start, (zero, zero), unroll=4)
+        return packed, pw, g0
+
+    packed, pw, g0 = lax.fori_loop(0, NXL, start, (zero,) * 3, unroll=4)
 
     def exchange(i, field, packed):
         vz[i] = packed
         copies = [
-            remote(field.at[NXL, inner], field.at[0, inner], sendv.at[i, 0], recvv.at[i, 0], {"gx": fwd["gx"]}),
-            remote(field.at[1, inner], field.at[NXL + 1, inner], sendv.at[i, 1], recvv.at[i, 1], {"gx": bwd["gx"]}),
-            remote(vyup.at[i], vyup_in.at[i], sendv.at[i, 2], recvv.at[i, 2], {"gy": fwd["gy"]}),
-            remote(vydn.at[i], vydn_in.at[i], sendv.at[i, 3], recvv.at[i, 3], {"gy": bwd["gy"]}),
-            remote(vz.at[i], vz_lo.at[i], sendv.at[i, 4], recvv.at[i, 4], {"gz": fwd["gz"]}),
-            remote(vz.at[i], vz_hi.at[i], sendv.at[i, 5], recvv.at[i, 5], {"gz": bwd["gz"]}),
+            Shift(field.at[NXL, inner], vx_in.at[i, 0], sendv.at[i, 0], recvv.at[i, 0], "gx", True),
+            Shift(field.at[1, inner], vx_in.at[i, 1], sendv.at[i, 1], recvv.at[i, 1], "gx", False),
+            Shift(vyup.at[i], vy_in.at[i, 0], sendv.at[i, 2], recvv.at[i, 2], "gy", True),
+            Shift(vydn.at[i], vy_in.at[i, 1], sendv.at[i, 3], recvv.at[i, 3], "gy", False),
+            Shift(vz.at[i], vz_lo.at[i], sendv.at[i, 4], recvv.at[i, 4], "gz", True),
+            Shift(vz.at[i], vz_hi.at[i], sendv.at[i, 5], recvv.at[i, 5], "gz", False),
         ]
         for copy in copies:
             copy.start()
         if i == 0:
             for copy in later:
                 copy.start()
+        sent.extend(copies)
+        heard(i)
+        if i < 2:
+            tell(i + 1)
+        else:
+            for d in range(1, RING):
+                pl.semaphore_signal(
+                    ready, inc=1, device_id={"gz": lax.rem(pos["gz"] + d, RING)}, device_id_type=MESH
+                )
+        return copies
+
+    def interior(i, field):
+        def plane_of(x, dot):
+            for k in range(BLOCKS):
+                r = TOP + 8 * k
+                rows, own = pl.ds(r, 8), pl.ds(8 * k, 8)
+                v = field[x + 1, rows]
+                q = (
+                    (wx[x, own] * (v - field[x, rows]) + wx[x + 1, own] * (v - field[x + 2, rows]))
+                    + (
+                        wyd[x, own] * (v - field[x + 1, pl.ds(r - 1, 8)])
+                        + wyu[x, own] * (v - field[x + 1, pl.ds(r + 1, 8)])
+                    )
+                    + (wzd[x, own] * (v - below(v, 0.0)) + wzu[x, own] * (v - above(v, 0.0)))
+                )
+                part[x, own] = q
+                dot = dot + v * q
+            return dot
+
+        return lax.fori_loop(0, NXL, plane_of, zero, unroll=4)
+
+    def arrive(i, copies):
         for copy in copies:
             copy.wait_recv()
-        sent.extend(copies)
-        clear_x((field,), (field,))
         vmix[i] = mix(vz_lo[i], vz_hi[i])
+
+    def join(i):
+        part[0] = part[0] - wx[0] * vx_in[i, 0]
+        part[NXL - 1] = part[NXL - 1] - wx[NXL] * vx_in[i, 1]
         for x in range(NXL):
             row = pl.ds(x, 1)
-            field[x + 1, pl.ds(TOP - 1, 1)] = jnp.where(low["gy"], 0.0, vyup_in[i, row])
-            field[x + 1, pl.ds(LAST + 1, 1)] = jnp.where(high["gy"], 0.0, vydn_in[i, row])
+            part[x, 0:1] = part[x, 0:1] - wyb[0, row] * vy_in[i, 0, row]
+            part[x, NYL - 1 : NYL] = part[x, NYL - 1 : NYL] - wyb[1, row] * vy_in[i, 1, row]
 
     def around(x, k, i, field):
         r = TOP + 8 * k
@@ -284,26 +356,20 @@
             (field[x, rows], field[x + 1, pl.ds(r - 1, 8)], below(v, edge)),
         )
 
-    def operate(x, k, i, field):
-        own = pl.ds(8 * k, 8)
-        v, (xp, yp, zp), (xm, ym, zm) = around(x, k, i, field)
-        image = (
-            (wx[x, own] * (v - xm) + wx[x + 1, own] * (v - xp))
-            + (wyd[x, own] * (v - ym) + wyu[x, own] * (v - yp))
-            + (wzd[x, own] * (v - zm) + wzu[x, own] * (v - zp))
-        )
-        return v, image
-
-    exchange(0, fv0, packed)
+    copies = exchange(0, fv0, packed)
+    interior(0, fv0)
+    arrive(0, copies)
+    join(0)
 
     def step0(x, carry):
         packed, h00, h01 = carry
         for k in range(BLOCKS):
-            own = pl.ds(8 * k, 8)
-            v, q = operate(x, k, 0, fv0)
+            own, rows = pl.ds(8 * k, 8), pl.ds(TOP + 8 * k, 8)
+            v = fv0[x + 1, rows]
+            q = part[x, own] - wzb[x, own] * place(x, k, vmix[0])
             w = minv[x, own] * q - v
             img[x, own] = q
-            fv1[x + 1, pl.ds(TOP + 8 * k, 8)] = w
+            fv1[x + 1, rows] = w
             packed = pick(x, k, w, packed)
             faces(1, x, k, w)
             h00 = h00 + v * q
@@ -311,37 +377,52 @@
         return packed, h00, h01
 
     packed, h00, h01 = lax.fori_loop(0, NXL, step0, (zero, zero, zero), unroll=4)
-    exchange(1, fv1, packed)
-    for d in range(1, RING):
-        pl.semaphore_signal(
-            ready, inc=1, device_id={"gz": lax.rem(pos["gz"] + d, RING)}, device_id_type=MESH
-        )
+    copies = exchange(1, fv1, packed)
+    interior(1, fv1)
+    arrive(1, copies)
+    join(1)
 
     def step1(x, carry):
-        packed, h02, h11, h12, g2 = carry
+        packed, h11, h12 = carry
+        for k in range(BLOCKS):
+            own, rows = pl.ds(8 * k, 8), pl.ds(TOP + 8 * k, 8)
+            v = fv1[x + 1, rows]
+            q = part[x, own] - wzb[x, own] * place(x, k, vmix[1])
+            w = minv[x, own] * q - v
+            fv2[x + 1, rows] = w
+            packed = pick(x, k, w, packed)
+            faces(2, x, k, w)
+            h11 = h11 + v * q
+            h12 = h12 + w * q
+        return packed, h11, h12
+
+    packed, h11, h12 = lax.fori_loop(0, NXL, step1, (zero,) * 3, unroll=4)
+    copies = exchange(2, fv2, packed)
+    inside = interior(2, fv2)
+
+    def dots(x, carry):
+        h02, g2 = carry
         for k in range(BLOCKS):
             own = pl.ds(8 * k, 8)
-            v, q = operate(x, k, 1, fv1)
-            w = minv[x, own] * q - v
-            fv2[x + 1, pl.ds(TOP + 8 * k, 8)] = w
-            packed = pick(x, k, w, packed)
-            faces(2, x, k, w)
-            h02 = h02 + w * img[x, own]
-            h11 = h11 + v * q
-            h12 = h12 + w * q
-            g2 = g2 + w * rhs[x, own]
-        return packed, h02, h11, h12, g2
-
-    packed, h02, h11, h12, g2 = lax.fori_loop(0, NXL, step1, (zero,) * 5, unroll=4)
-    exchange(2, fv2, packed)
-
-    def step2(x, h22):
-        for k in range(BLOCKS):
-            v, q = operate(x, k, 2, fv2)
-            h22 = h22 + v * q
-        return h22
-
-    h22 = lax.fori_loop(0, NXL, step2, zero, unroll=4)
+            v = fv2[x + 1, pl.ds(TOP + 8 * k, 8)]
+            h02 = h02 + v * img[x, own]
+            g2 = g2 + v * rhs[x, own]
+        return h02, g2
+
+    h02, g2 = lax.fori_loop(0, NXL, dots, (zero, zero), unroll=4)
+    arrive(2, copies)
+    outside = pw * packed * vmix[2]
+    for k in range(BLOCKS):
+        own, rows = pl.ds(8 * k, 8), pl.ds(TOP + 8 * k, 8)
+        outside = outside + (
+            wx[0, own] * fv2[1, rows] * vx_in[2, 0, own] + wx[NXL, own] * fv2[NXL, rows] * vx_in[2, 1, own]
+        )
+    for half_x in range(NXL // 8):
+        xs = pl.ds(8 * half_x, 8)
+        outside = outside + (
+            wyb[0, xs] * vydn[2, xs] * vy_in[2, 0, xs] + wyb[1, xs] * vyup[2, xs] * vy_in[2, 1, xs]
+        )
+    h22 = inside - outside
 
     sub = lax.broadcasted_iota(jnp.int32, (8, NZL), 0)
     level = [(value, None) for value in (g0, g2, h00, h01, h02, h11, h12, h22)]
@@ -386,12 +467,17 @@
         if phase == 0:
             for copy in later:
                 copy.wait_recv()
-            clear_x((fp,), (fp,))
             zmix[1] = mix(pz_lo[...], pz_hi[...])
+            for i, field in enumerate((fv0, fv1, fv2)):
+                field[0, inner] = vx_in[i, 0]
+                field[NXL + 1, inner] = vx_in[i, 1]
             for x in range(NXL):
                 lrow = pl.ds(x, 1)
-                fp[x + 1, pl.ds(TOP - 1, 1)] = jnp.where(low["gy"], 0.0, pyup_in[lrow])
-                fp[x + 1, pl.ds(LAST + 1, 1)] = jnp.where(high["gy"], 0.0, pydn_in[lrow])
+                fp[x + 1, pl.ds(TOP - 1, 1)] = pyup_in[lrow]
+                fp[x + 1, pl.ds(LAST + 1, 1)] = pydn_in[lrow]
+                for i, field in enumerate((fv0, fv1, fv2)):
+                    field[x + 1, pl.ds(TOP - 1, 1)] = vy_in[i, 0, lrow]
+                    field[x + 1, pl.ds(LAST + 1, 1)] = vy_in[i, 1, lrow]
 
             def terms(x, carry):
                 for k in range(BLOCKS):
@@ -531,12 +617,16 @@
             pltpu.VMEM((NXL, NYL, NZL), jnp.int32),
             *[field] * 8,
             pltpu.VMEM((NXL + 1, NYL, NZL), F32),
-            *[block] * 7,
+            *[block] * 5,
+            pltpu.VMEM((2, NXL, NZL), F32),
+            *[block] * 4,
             pltpu.VMEM((3, 3, NXL, NYL, NZL), F32),
             pltpu.VMEM((4, NXL, NYL, NZL), F32),
             pltpu.VMEM((2, NXL, NZL), F32), flat, pltpu.VMEM((2, NXL, NZL), F32), flat,
             *[flat] * 4,
-            *[flats] * 4,
+            *[flats] * 2,
+            pltpu.VMEM((3, 2, NXL, NZL), F32),
+            pltpu.VMEM((3, 2, NYL, NZL), F32),
             *[pltpu.VMEM((2, 8, NZL), F32)] * 3,
             *[tile] * 3,
             *[tiles] * 5,
@@ -545,6 +635,7 @@
             dma((13,)), dma((13,)), dma((3, 6)), dma((3, 6)),
             dma((len(PHASES),)), dma((len(PHASES),)),
             pltpu.SemaphoreType.REGULAR,
+            pltpu.SemaphoreType.REGULAR((3, 3)),
         ],
         compiler_params=pltpu.CompilerParams(
             collective_id=0, has_side_effects=True, vmem_limit_bytes=24 * 1024 * 1024

time: 43.3 us -> 42.4 us (0.979)
  Pallas kernels: 42.5 us -> 41.6 us
    pallas_call x1, Pallas kernels: 41.5 us -> 40.7 us  [on_device(): pl.pallas_call(body, out_shape=out_shape, in_specs=[in_hbm] * 3, out_spec...]
where the time goes in v3:
time: 42.4 us; the launch traced here: 42.3 us
  Pallas kernels  41.6 us (98%)
  between operations  0.64 us (2%)
    pallas_call x1, Pallas kernels, on_device(): pl.pallas_call(body, out_shape=out_shape, in_specs=[in_hbm] * 3, out_spec...  40.7 us
    pallas_call x1, Pallas kernels, on_device(): pl.pallas_call(save, out_shape=out_shape, in_specs=[in_vmem] * 2, out_spe...  0.98 us

profile of v3, /device:TPU:1, one launch (start us, length us, event | category | flops | bytes accessed | tf_op | source)
XLA Modules:
  0.0 42.3 jit_solution(8941814426926162243)
XLA Ops:
  0.6 40.7 %projection_adjoint.1 = (f32[3,16,32,128]{3,2,1,0:T(8,128)S(1)}, f32[16,32,128]{2,1,0:T(8,128)S(1)}) custom-call(s32[16,32,128]{2,1,0:T(8,128)} %mask_hbm.1, f32[16,32,128]{2,1,0:T(8,128)} %press_hbm.1, f32[3,16,32,128]{3,2,1,0:T(8,128)} %vel_hbm.1), custom_call_target="tpu_custom_call" | custom-call | tf_op jit(solution)/shard_map/projection_adjoint/pallas_call | solution.py:611
  41.3 1.0 %save.1 = (f32[3,16,32,128]{3,2,1,0:T(8,128)}, f32[16,32,128]{2,1,0:T(8,128)}) custom-call(f32[3,16,32,128]{3,2,1,0:T(8,128)S(1)} %get-tuple-element.4.ustar, f32[16,32,128]{2,1,0:T(8,128)S(1)} %get-tuple-element.5.coef), custom_call_target="tpu_custom_call" | custom-call | tf_op jit(solution)/shard_map/save/pallas_call | solution.py:645

commit v4 on v3

--- a/solution.py
+++ b/solution.py
@@ -80,32 +80,42 @@
 def body(
     mask_hbm, press_hbm, vel_hbm, out_u, out_c,
     mask, fc, fp, fu0, fu1, fu2, fv0, fv1, fv2,
-    wx, wyu, wyd, wzu, wzd, wzb, wyb, minv, rhs, img, part,
+    wx, wyu, wyd, wzu, wzd, wyb, minv, rhs, img, part,
     grads, bases,
-    yup, ydn, yup_in, ydn_in, pyup, pydn, pyup_in, pydn_in, vyup, vydn, vy_in, vx_in,
-    zup, zin_lo, zin_hi, pz, pz_lo, pz_hi, zmix, vz, vz_lo, vz_hi, vmix,
+    kx_out, kx_in, ky_out, ky_in, kz_out, kz_lo, kz_hi,
+    tx_out, tx_in, ty_out, ty_in, tz_out, tz_lo, tz_hi,
+    dxy, dxz, dyz, dyz_rows,
+    cyup, cydn, uyup, cx_in, ux_in, cy_in, uy_in, pyup, pydn, pyup_in, pydn_in, vyup, vydn, vy_in, vx_in,
+    cz, cz_lo, cz_hi, uz, uz_lo, pz, pz_lo, pz_hi, zmix, vz, vz_lo, vz_hi, vmix,
     sums,
     load_sem,
-    send1, recv1, sendv, recvv, sendr, recvr, ready, token,
+    send1, recv1, sendv, recvv, sendr, recvr, ready, token, sendk, recvk,
 ):
     pos = {axis: lax.axis_index(axis) for axis in AXES}
     fwd = {axis: lax.rem(pos[axis] + 1, RING) for axis in AXES}
     bwd = {axis: lax.rem(pos[axis] + RING - 1, RING) for axis in AXES}
     lane = lax.broadcasted_iota(jnp.int32, (8, NZL), 1)
+    sub = lax.broadcasted_iota(jnp.int32, (8, NZL), 0)
     half = lane // 2
     even = lane - 2 * half == 0
     first = lane == 0
     final = lane == NZL - 1
+    border = jnp.logical_or(first, final)
 
     low = {axis: pos[axis] == 0 for axis in AXES}
     high = {axis: pos[axis] == RING - 1 for axis in AXES}
 
     class Shift:
-        def __init__(self, src, dst, send, recv, axis, up):
-            other = fwd[axis] if up else bwd[axis]
-            self.copy = remote(src, dst, send, recv, {axis: other})
-            self.sends = jnp.logical_not(high[axis] if up else low[axis])
-            self.receives = jnp.logical_not(low[axis] if up else high[axis])
+        def __init__(self, src, dst, send, recv, *moves):
+            moves = tuple(zip(moves[::2], moves[1::2]))
+            device = {axis: fwd[axis] if up else bwd[axis] for axis, up in moves}
+            self.copy = remote(src, dst, send, recv, device)
+            self.sends = self.receives = None
+            for axis, up in moves:
+                sends = jnp.logical_not(high[axis] if up else low[axis])
+                receives = jnp.logical_not(low[axis] if up else high[axis])
+                self.sends = sends if self.sends is None else jnp.logical_and(self.sends, sends)
+                self.receives = receives if self.receives is None else jnp.logical_and(self.receives, receives)
 
         def start(self):
             pl.when(self.sends)(lambda: self.copy.start())
@@ -135,7 +145,7 @@
 
     cells = (pl.ds(1, NXL), pl.ds(TOP, NYL))
     loads = [pltpu.make_async_copy(mask_hbm, mask, load_sem.at[0])]
-    for i, field in enumerate((fu0, fu1, fu2)):
+    for i, field in ((2, fu2), (1, fu1), (0, fu0)):
         loads.append(pltpu.make_async_copy(vel_hbm.at[i], field.at[cells], load_sem.at[1 + i]))
     loads.append(pltpu.make_async_copy(press_hbm, fp.at[cells], load_sem.at[4]))
     for load in loads:
@@ -149,19 +159,21 @@
         field[0, inner] = plane
         field[NXL + 1, inner] = plane
     for x in range(1, NXL + 1):
-        for field in (fv0, fv1, fv2):
+        fu1[x, pl.ds(TOP - 1, 1)] = line
+        for field in (fc, fv0, fv1, fv2):
             field[x, pl.ds(TOP - 1, 1)] = line
             field[x, pl.ds(LAST + 1, 1)] = line
-    for buffer in (yup_in, ydn_in, pyup_in, pydn_in, vy_in, vx_in, zin_lo, zin_hi, pz_lo, pz_hi, vz_lo, vz_hi):
+    for buffer in (
+        cx_in, ux_in, cy_in, uy_in, pyup_in, pydn_in, vy_in, vx_in,
+        cz_lo, cz_hi, uz_lo, pz_lo, pz_hi, vz_lo, vz_hi,
+        kx_in, ky_in, kz_lo, kz_hi, tx_in, ty_in, tz_lo, tz_hi, dxy, dxz, dyz, dyz_rows, kx_out, ky_out,
+    ):
         buffer[...] = jnp.zeros(buffer.shape, F32)
 
     barrier = pltpu.get_barrier_semaphore()
     for axis in AXES:
         for other in (fwd[axis], bwd[axis]):
             pl.semaphore_signal(barrier, inc=1, device_id={axis: other}, device_id_type=MESH)
-    for load in loads:
-        load.wait()
-
     def pick(x, k, value, packed):
         return jnp.where(half == BLOCKS * x + k, roll(value, 2 * BLOCKS * x + 2 * k + 1, 1), packed)
 
@@ -174,68 +186,133 @@
     def below(value, edge):
         return jnp.where(first, edge, roll(value, 1, 1))
 
-    def prepare(x, carry):
-        pc, pp, pu = carry
-        for k in range(BLOCKS):
-            rows = pl.ds(TOP + 8 * k, 8)
+    loads[0].wait()
+
+    def prepare(x, packed):
+        for k in range(BLOCKS):
             phase = mask[x, pl.ds(8 * k, 8)]
             c = jnp.where(phase == 0, 8.0, jnp.where(phase == 1, 1.0, 2.0)).astype(F32)
-            fc[x + 1, rows] = c
-            pc = pick(x, k, c, pc)
-            pp = pick(x, k, fp[x + 1, rows], pp)
-            pu = pick(x, k, fu2[x + 1, rows], pu)
+            fc[x + 1, pl.ds(TOP + 8 * k, 8)] = c
+            packed = pick(x, k, c, packed)
             if k == 0:
-                ydn[pl.ds(x, 1)] = c[0:1]
-                pydn[pl.ds(x, 1)] = fp[x + 1, pl.ds(TOP, 1)]
+                cydn[pl.ds(x, 1)] = c[0:1]
             if k == BLOCKS - 1:
-                yup[0, pl.ds(x, 1)] = c[7:8]
-                pyup[pl.ds(x, 1)] = fp[x + 1, pl.ds(LAST, 1)]
-                yup[1, pl.ds(x, 1)] = fu1[x + 1, pl.ds(LAST, 1)]
-        return pc, pp, pu
-
-    pc, pp, pu = lax.fori_loop(0, NXL, prepare, (zero, zero, zero), unroll=4)
-    zup[0] = pc
-    zup[1] = pu
+                cyup[pl.ds(x, 1)] = c[7:8]
+        return packed
+
+    cz[...] = lax.fori_loop(0, NXL, prepare, zero, unroll=4)
+    pl.semaphore_wait(barrier, 6)
+    sent = []
+
+    def launch(copies):
+        for copy in copies:
+            copy.start()
+        sent.extend(copies)
+        return copies
+
+    round1 = launch([
+        Shift(fc.at[NXL, inner], cx_in.at[0], send1.at[0], recv1.at[0], "gx", True),
+        Shift(fc.at[1, inner], cx_in.at[1], send1.at[1], recv1.at[1], "gx", False),
+        Shift(cyup, cy_in.at[0], send1.at[2], recv1.at[2], "gy", True),
+        Shift(cydn, cy_in.at[1], send1.at[3], recv1.at[3], "gy", False),
+        Shift(cz, cz_lo, send1.at[4], recv1.at[4], "gz", True),
+        Shift(cz, cz_hi, send1.at[5], recv1.at[5], "gz", False),
+    ])
+    for load in loads[1:4]:
+        load.wait()
+
+    def velocity(x, packed):
+        for k in range(BLOCKS):
+            packed = pick(x, k, fu2[x + 1, pl.ds(TOP + 8 * k, 8)], packed)
+        uyup[pl.ds(x, 1)] = fu1[x + 1, pl.ds(LAST, 1)]
+        return packed
+
+    uz[...] = lax.fori_loop(0, NXL, velocity, zero, unroll=4)
+    round1 += launch([
+        Shift(uz, uz_lo, send1.at[6], recv1.at[6], "gz", True),
+        Shift(fu0.at[NXL, inner], ux_in, send1.at[7], recv1.at[7], "gx", True),
+        Shift(uyup, uy_in, send1.at[8], recv1.at[8], "gy", True),
+    ])
+    tell(0)
+    loads[4].wait()
+
+    def mix(lo, hi):
+        return jnp.where(even, roll(hi, NZL - 1, 1), roll(lo, 1, 1))
+
+    def weigh(x, carry):
+        pw, pp = carry
+        for k in range(BLOCKS):
+            r = TOP + 8 * k
+            rows, own = pl.ds(r, 8), pl.ds(8 * k, 8)
+            c = fc[x + 1, rows]
+            xu = 0.5 * (c + fc[x + 2, rows])
+            xd = 0.5 * (c + fc[x, rows])
+            yu = 0.5 * (c + fc[x + 1, pl.ds(r + 1, 8)])
+            yd = 0.5 * (c + fc[x + 1, pl.ds(r - 1, 8)])
+            zu = 0.5 * (c + above(c, 0.0))
+            zd = 0.5 * (c + below(c, 0.0))
+            u2 = fu2[x + 1, rows]
+            wx[x + 1, own] = xu
+            wyu[x, own] = yu
+            wyd[x, own] = yd
+            wzu[x, own] = zu
+            wzd[x, own] = zd
+            minv[x, own] = (xd + xu) + (yd + yu) + (zd + zu)
+            rhs[x, own] = (
+                (xu * fu0[x + 1, rows] - xd * fu0[x, rows])
+                + (yu * fu1[x + 1, rows] - yd * fu1[x + 1, pl.ds(r - 1, 8)])
+                + (zu * u2 - zd * below(u2, 0.0))
+            )
+            pw = pick(x, k, jnp.where(first, zd, zu), pw)
+            p = fp[x + 1, rows]
+            pp = pick(x, k, p, pp)
+            if k == 0:
+                pydn[pl.ds(x, 1)] = p[0:1]
+            if k == BLOCKS - 1:
+                pyup[pl.ds(x, 1)] = p[7:8]
+        return pw, pp
+
+    pw, pp = lax.fori_loop(0, NXL, weigh, (zero, zero), unroll=4)
     pz[...] = pp
-
-    pl.semaphore_wait(barrier, 6)
-
-    round1 = [
-        Shift(fc.at[NXL, inner], fc.at[0, inner], send1.at[0], recv1.at[0], "gx", True),
-        Shift(fc.at[1, inner], fc.at[NXL + 1, inner], send1.at[1], recv1.at[1], "gx", False),
-        Shift(yup, yup_in, send1.at[2], recv1.at[2], "gy", True),
-        Shift(ydn, ydn_in, send1.at[3], recv1.at[3], "gy", False),
-        Shift(zup, zin_lo, send1.at[4], recv1.at[4], "gz", True),
-        Shift(zup, zin_hi, send1.at[5], recv1.at[5], "gz", False),
-        Shift(fu0.at[NXL, inner], fu0.at[0, inner], send1.at[6], recv1.at[6], "gx", True),
-    ]
-    for copy in round1:
-        copy.start()
-    tell(0)
     later = [
-        Shift(fp.at[NXL, inner], fp.at[0, inner], send1.at[7], recv1.at[7], "gx", True),
-        Shift(fp.at[1, inner], fp.at[NXL + 1, inner], send1.at[8], recv1.at[8], "gx", False),
-        Shift(pyup, pyup_in, send1.at[9], recv1.at[9], "gy", True),
-        Shift(pydn, pydn_in, send1.at[10], recv1.at[10], "gy", False),
-        Shift(pz, pz_lo, send1.at[11], recv1.at[11], "gz", True),
-        Shift(pz, pz_hi, send1.at[12], recv1.at[12], "gz", False),
+        Shift(fp.at[NXL, inner], fp.at[0, inner], send1.at[9], recv1.at[9], "gx", True),
+        Shift(fp.at[1, inner], fp.at[NXL + 1, inner], send1.at[10], recv1.at[10], "gx", False),
+        Shift(pyup, pyup_in, send1.at[11], recv1.at[11], "gy", True),
+        Shift(pydn, pydn_in, send1.at[12], recv1.at[12], "gy", False),
+        Shift(pz, pz_lo, send1.at[13], recv1.at[13], "gz", True),
+        Shift(pz, pz_hi, send1.at[14], recv1.at[14], "gz", False),
     ]
     for copy in round1:
         copy.wait_recv()
-    sent = round1 + later
-
-    def mix(lo, hi):
-        return jnp.where(even, roll(hi, NZL - 1, 1), roll(lo, 1, 1))
-
-    zmix[0] = mix(zin_lo[0], zin_hi[0])
-    zmix[2] = mix(zin_lo[1], zin_hi[1])
+
+    h = 0.5 * cx_in[0]
+    w = 0.5 * fc[1, inner] + h
+    wx[0] = w
+    minv[0] = minv[0] + h
+    rhs[0] = rhs[0] - w * ux_in[...]
+    h = 0.5 * cx_in[1]
+    wx[NXL] = wx[NXL] + h
+    minv[NXL - 1] = minv[NXL - 1] + h
+    rhs[NXL - 1] = rhs[NXL - 1] + h * fu0[NXL, inner]
     for x in range(NXL):
-        row = pl.ds(x, 1)
-        fc[x + 1, pl.ds(TOP - 1, 1)] = yup_in[0, row]
-        fu1[x + 1, pl.ds(TOP - 1, 1)] = yup_in[1, row]
-        fc[x + 1, pl.ds(LAST + 1, 1)] = ydn_in[row]
-
-    wx[0] = 0.5 * (fc[0, inner] + fc[1, inner])
+        row, top, bottom = pl.ds(x, 1), pl.ds(0, 1), pl.ds(NYL - 1, 1)
+        h = 0.5 * cy_in[0, row]
+        w = wyd[x, top] + h
+        wyd[x, top] = w
+        wyb[0, row] = w
+        minv[x, top] = minv[x, top] + h
+        rhs[x, top] = rhs[x, top] - w * uy_in[row]
+        h = 0.5 * cy_in[1, row]
+        w = wyu[x, bottom] + h
+        wyu[x, bottom] = w
+        wyb[1, row] = w
+        minv[x, bottom] = minv[x, bottom] + h
+        rhs[x, bottom] = rhs[x, bottom] + h * uyup[row]
+    hz = 0.5 * mix(cz_lo[...], cz_hi[...])
+    pw = pw + hz
+    uz_mix = roll(uz_lo[...], 1, 1)
+    zmix[1] = uz_mix
+    pr = jnp.where(even, hz * uz[...], -pw * uz_mix)
 
     def faces(i, x, k, value):
         if k == 0:
@@ -244,47 +321,21 @@
             vyup[i, pl.ds(x, 1)] = value[7:8]
 
     def start(x, carry):
-        packed, pw, g0 = carry
-        for k in range(BLOCKS):
-            r = TOP + 8 * k
-            rows, own = pl.ds(r, 8), pl.ds(8 * k, 8)
-            c = fc[x + 1, rows]
-            edge = place(x, k, zmix[0])
-            xu = 0.5 * (c + fc[x + 2, rows])
-            xd = wx[x, own]
-            yu = 0.5 * (c + fc[x + 1, pl.ds(r + 1, 8)])
-            yd = 0.5 * (c + fc[x + 1, pl.ds(r - 1, 8)])
-            zu = 0.5 * (c + above(c, edge))
-            zd = 0.5 * (c + below(c, edge))
-            m = 1.0 / ((xd + xu) + (yd + yu) + (zd + zu))
-            u2 = fu2[x + 1, rows]
-            r0 = (
-                (xu * fu0[x + 1, rows] - xd * fu0[x, rows])
-                + (yu * fu1[x + 1, rows] - yd * fu1[x + 1, pl.ds(r - 1, 8)])
-                + (zu * u2 - zd * below(u2, place(x, k, zmix[2])))
-            )
+        packed, g0 = carry
+        for k in range(BLOCKS):
+            own = pl.ds(8 * k, 8)
+            m = 1.0 / (minv[x, own] + jnp.where(border, place(x, k, hz), 0.0))
+            r0 = rhs[x, own] + jnp.where(border, place(x, k, pr), 0.0)
             v = m * r0
-            wx[x + 1, own] = xu
-            wyu[x, own] = yu
-            wyd[x, own] = yd
-            wzu[x, own] = zu
-            wzd[x, own] = zd
             minv[x, own] = m
             rhs[x, own] = r0
-            zb = jnp.where(first, zd, jnp.where(final, zu, 0.0))
-            wzb[x, own] = zb
-            pw = pick(x, k, zb, pw)
-            if k == 0:
-                wyb[0, pl.ds(x, 1)] = yd[0:1]
-            if k == BLOCKS - 1:
-                wyb[1, pl.ds(x, 1)] = yu[7:8]
-            fv0[x + 1, rows] = v
+            fv0[x + 1, pl.ds(TOP + 8 * k, 8)] = v
             packed = pick(x, k, v, packed)
             faces(0, x, k, v)
             g0 = g0 + v * r0
-        return packed, pw, g0
-
-    packed, pw, g0 = lax.fori_loop(0, NXL, start, (zero,) * 3, unroll=4)
+        return packed, g0
+
+    packed, g0 = lax.fori_loop(0, NXL, start, (zero,) * 2, unroll=4)
 
     def exchange(i, field, packed):
         vz[i] = packed
@@ -296,24 +347,16 @@
             Shift(vz.at[i], vz_lo.at[i], sendv.at[i, 4], recvv.at[i, 4], "gz", True),
             Shift(vz.at[i], vz_hi.at[i], sendv.at[i, 5], recvv.at[i, 5], "gz", False),
         ]
-        for copy in copies:
-            copy.start()
+        launch(copies)
         if i == 0:
-            for copy in later:
-                copy.start()
-        sent.extend(copies)
+            launch(later)
         heard(i)
-        if i < 2:
-            tell(i + 1)
-        else:
-            for d in range(1, RING):
-                pl.semaphore_signal(
-                    ready, inc=1, device_id={"gz": lax.rem(pos["gz"] + d, RING)}, device_id_type=MESH
-                )
+        tell(i + 1)
         return copies
 
     def interior(i, field):
-        def plane_of(x, dot):
+        def plane_of(x, carry):
+            dot, packed = carry
             for k in range(BLOCKS):
                 r = TOP + 8 * k
                 rows, own = pl.ds(r, 8), pl.ds(8 * k, 8)
@@ -327,15 +370,19 @@
                     + (wzd[x, own] * (v - below(v, 0.0)) + wzu[x, own] * (v - above(v, 0.0)))
                 )
                 part[x, own] = q
-                dot = dot + v * q
-            return dot
-
-        return lax.fori_loop(0, NXL, plane_of, zero, unroll=4)
+                if i == 1:
+                    packed = pick(x, k, q, packed)
+                if i == 2:
+                    dot = dot + v * q
+            return dot, packed
+
+        return lax.fori_loop(0, NXL, plane_of, (zero, zero), unroll=4)
 
     def arrive(i, copies):
         for copy in copies:
             copy.wait_recv()
         vmix[i] = mix(vz_lo[i], vz_hi[i])
+        return pw * vmix[i] - hz * vz[i]
 
     def join(i):
         part[0] = part[0] - wx[0] * vx_in[i, 0]
@@ -358,7 +405,51 @@
 
     copies = exchange(0, fv0, packed)
     interior(0, fv0)
-    arrive(0, copies)
+
+    def at_border(x, k, mixed):
+        return jnp.where(border, place(x, k, mixed), 0.0)
+
+    def spread_rows(x, carry):
+        pm, py = carry
+        row = pl.ds(x, 1)
+        for k in range(BLOCKS):
+            own = pl.ds(8 * k, 8)
+            m = minv[x, own]
+            pm = pick(x, k, m, pm)
+            if k == 0:
+                py = pick(x, k, jnp.where(sub == 0, wyd[x, own], 0.0), py)
+                ky_out[0, row] = m[0:1] * wyb[0, row]
+                ky_out[0, pl.ds(NXL + x, 1)] = (m * at_border(x, k, pw))[0:1]
+            if k == BLOCKS - 1:
+                py = pick(x, k, jnp.where(sub == 7, wyu[x, own], 0.0), py)
+                ky_out[1, row] = m[7:8] * wyb[1, row]
+                ky_out[1, pl.ds(NXL + x, 1)] = (m * at_border(x, k, pw))[7:8]
+        return pm, py
+
+    pm, py = lax.fori_loop(0, NXL, spread_rows, (zero, zero))
+    px = zero
+    for side, p, wp in ((0, 0, 0), (1, NXL - 1, NXL)):
+        for k in range(BLOCKS):
+            own = pl.ds(8 * k, 8)
+            px = pick(p, k, wx[wp, own], px)
+            kx_out[side, own] = minv[p, own] * wx[wp, own]
+            kx_out[side, pl.ds(NYL + 8 * k, 8)] = minv[p, own] * at_border(p, k, pw)
+        for end, y in ((0, 0), (1, NYL - 1)):
+            m = minv[p, pl.ds(y, 1)]
+            kx_out[side, pl.ds(2 * NYL + end, 1)] = m * wyb[end, pl.ds(p, 1)]
+            ky_out[end, pl.ds(2 * NXL + side, 1)] = m * wx[wp, pl.ds(y, 1)]
+    kz_out[0] = pm * pw
+    kz_out[1] = pm * px
+    kz_out[2] = pm * py
+    statics = launch([
+        Shift(kx_out.at[1], kx_in.at[0], sendk.at[0], recvk.at[0], "gx", True),
+        Shift(kx_out.at[0], kx_in.at[1], sendk.at[1], recvk.at[1], "gx", False),
+        Shift(ky_out.at[1], ky_in.at[0], sendk.at[2], recvk.at[2], "gy", True),
+        Shift(ky_out.at[0], ky_in.at[1], sendk.at[3], recvk.at[3], "gy", False),
+        Shift(kz_out, kz_lo, sendk.at[4], recvk.at[4], "gz", True),
+        Shift(kz_out, kz_hi, sendk.at[5], recvk.at[5], "gz", False),
+    ])
+    pq = arrive(0, copies)
     join(0)
 
     def step0(x, carry):
@@ -366,7 +457,7 @@
         for k in range(BLOCKS):
             own, rows = pl.ds(8 * k, 8), pl.ds(TOP + 8 * k, 8)
             v = fv0[x + 1, rows]
-            q = part[x, own] - wzb[x, own] * place(x, k, vmix[0])
+            q = part[x, own] - jnp.where(border, place(x, k, pq), 0.0)
             w = minv[x, own] * q - v
             img[x, own] = q
             fv1[x + 1, rows] = w
@@ -378,40 +469,118 @@
 
     packed, h00, h01 = lax.fori_loop(0, NXL, step0, (zero, zero, zero), unroll=4)
     copies = exchange(1, fv1, packed)
-    interior(1, fv1)
-    arrive(1, copies)
+    diagonal = []
+    n = 12
+    for a, up_a in enumerate((True, False)):
+        for b, up_b in enumerate((True, False)):
+            slot = 2 * a + b
+            rows_b = (vyup if up_b else vydn).at[1]
+            rows_a = (vyup if up_a else vydn).at[1]
+            for src, dst, moves in (
+                (rows_b, dxy, ("gx", up_a, "gy", up_b)),
+                (vz.at[1], dxz, ("gx", up_a, "gz", up_b)),
+                (vz.at[1], dyz, ("gy", up_a, "gz", up_b)),
+                (rows_a, dyz_rows, ("gy", up_a, "gz", up_b)),
+            ):
+                diagonal.append(Shift(src, dst.at[slot], sendk.at[n], recvk.at[n], *moves))
+                n += 1
+    launch(diagonal)
+    _, packed_part = interior(1, fv1)
+    hv = hz * vz[1]
+    tz_out[...] = pm * (packed_part + hv) - vz[1]
+    for side, p in ((0, 0), (1, NXL - 1)):
+        for k in range(BLOCKS):
+            own = pl.ds(8 * k, 8)
+            tx_out[side, own] = (
+                minv[p, own] * (part[p, own] + at_border(p, k, hv)) - fv1[p + 1, pl.ds(TOP + 8 * k, 8)]
+            )
+    for x in range(NXL):
+        row = pl.ds(x, 1)
+        for side, k, y, r in ((0, 0, 0, 0), (1, BLOCKS - 1, NYL - 1, 7)):
+            own = (vydn if side == 0 else vyup)[1, row]
+            at = pl.ds(y, 1)
+            ty_out[side, row] = minv[x, at] * (part[x, at] + at_border(x, k, hv)[r : r + 1]) - own
+    partial = launch([
+        Shift(tx_out.at[1], tx_in.at[0], sendk.at[6], recvk.at[6], "gx", True),
+        Shift(tx_out.at[0], tx_in.at[1], sendk.at[7], recvk.at[7], "gx", False),
+        Shift(ty_out.at[1], ty_in.at[0], sendk.at[8], recvk.at[8], "gy", True),
+        Shift(ty_out.at[0], ty_in.at[1], sendk.at[9], recvk.at[9], "gy", False),
+        Shift(tz_out, tz_lo, sendk.at[10], recvk.at[10], "gz", True),
+        Shift(tz_out, tz_hi, sendk.at[11], recvk.at[11], "gz", False),
+    ])
+    pq = arrive(1, copies)
     join(1)
 
     def step1(x, carry):
-        packed, h11, h12 = carry
+        packed, h11, h12, h02, g2 = carry
         for k in range(BLOCKS):
             own, rows = pl.ds(8 * k, 8), pl.ds(TOP + 8 * k, 8)
             v = fv1[x + 1, rows]
-            q = part[x, own] - wzb[x, own] * place(x, k, vmix[1])
+            q = part[x, own] - jnp.where(border, place(x, k, pq), 0.0)
             w = minv[x, own] * q - v
             fv2[x + 1, rows] = w
             packed = pick(x, k, w, packed)
             faces(2, x, k, w)
             h11 = h11 + v * q
             h12 = h12 + w * q
-        return packed, h11, h12
-
-    packed, h11, h12 = lax.fori_loop(0, NXL, step1, (zero,) * 3, unroll=4)
-    copies = exchange(2, fv2, packed)
-    inside = interior(2, fv2)
-
-    def dots(x, carry):
-        h02, g2 = carry
+            h02 = h02 + w * img[x, own]
+            g2 = g2 + w * rhs[x, own]
+        return packed, h11, h12, h02, g2
+
+    packed, h11, h12, h02, g2 = lax.fori_loop(0, NXL, step1, (zero,) * 5, unroll=4)
+    inside, _ = interior(2, fv2)
+    heard(2)
+    for d in range(1, RING):
+        pl.semaphore_signal(
+            ready, inc=1, device_id={"gz": lax.rem(pos["gz"] + d, RING)}, device_id_type=MESH
+        )
+    for copy in statics + partial + diagonal:
+        copy.wait_recv()
+    mixed_x = [mix(dxz[2 * side], dxz[2 * side + 1]) for side in (0, 1)]
+    mixed_y = [mix(dyz[2 * side], dyz[2 * side + 1]) for side in (0, 1)]
+    for side, p, mine in ((0, NXL - 1, 1), (1, 0, NXL)):
         for k in range(BLOCKS):
             own = pl.ds(8 * k, 8)
-            v = fv2[x + 1, pl.ds(TOP + 8 * k, 8)]
-            h02 = h02 + v * img[x, own]
-            g2 = g2 + v * rhs[x, own]
-        return h02, g2
-
-    h02, g2 = lax.fori_loop(0, NXL, dots, (zero, zero), unroll=4)
-    arrive(2, copies)
-    outside = pw * packed * vmix[2]
+            vx_in[2, side, own] = (
+                tx_in[side, own]
+                - kx_in[side, own] * fv1[mine, pl.ds(TOP + 8 * k, 8)]
+                - kx_in[side, pl.ds(NYL + 8 * k, 8)] * place(p, k, mixed_x[side])
+            )
+        for end, y in ((0, 0), (1, NYL - 1)):
+            at = pl.ds(y, 1)
+            vx_in[2, side, at] = vx_in[2, side, at] - (
+                kx_in[side, pl.ds(2 * NYL + end, 1)] * dxy[2 * side + end, pl.ds(p, 1)]
+            )
+    for side in (0, 1):
+        own_rows = vydn if side == 0 else vyup
+        for block in range(NXL // 8):
+            xs = pl.ds(8 * block, 8)
+            beside = jnp.where(
+                first, roll(dyz_rows[2 * side, xs], 1, 1), roll(dyz_rows[2 * side + 1, xs], NZL - 1, 1)
+            )
+            vy_in[2, side, xs] = (
+                ty_in[side, xs]
+                - ky_in[side, xs] * own_rows[1, xs]
+                - ky_in[side, pl.ds(NXL + 8 * block, 8)] * beside
+            )
+        for end, x, far in ((0, 0, NXL - 1), (1, NXL - 1, 0)):
+            at = pl.ds(x, 1)
+            vy_in[2, side, at] = vy_in[2, side, at] - (
+                ky_in[side, pl.ds(2 * NXL + end, 1)] * dxy[2 * end + side, pl.ds(far, 1)]
+            )
+    beside_x = jnp.where(lane < 64, roll(mixed_x[0], 2 * BLOCKS, 1), roll(mixed_x[1], NZL - 2 * BLOCKS, 1))
+    step_k = 2 * (BLOCKS - 1)
+    beside_y = jnp.where(
+        sub == 0,
+        roll(roll(mixed_y[0], NZL - step_k, 1), 1, 0),
+        roll(roll(mixed_y[1], step_k, 1), 7, 0),
+    )
+    kz = [mix(kz_lo[i], kz_hi[i]) for i in range(3)]
+    vmix[2] = (
+        mix(tz_lo[...], tz_hi[...]) - kz[0] * vz[1] - kz[1] * beside_x - kz[2] * beside_y
+    )
+    pq = pw * vmix[2] - hz * packed
+    outside = packed * pq
     for k in range(BLOCKS):
         own, rows = pl.ds(8 * k, 8), pl.ds(TOP + 8 * k, 8)
         outside = outside + (
@@ -424,7 +593,6 @@
         )
     h22 = inside - outside
 
-    sub = lax.broadcasted_iota(jnp.int32, (8, NZL), 0)
     level = [(value, None) for value in (g0, g2, h00, h01, h02, h11, h12, h22)]
     for width in (4, 2, 1):
         keep = lax.rem(sub // width, 2) == 0
@@ -467,12 +635,14 @@
         if phase == 0:
             for copy in later:
                 copy.wait_recv()
-            zmix[1] = mix(pz_lo[...], pz_hi[...])
+            zmix[0] = mix(pz_lo[...], pz_hi[...])
+            fu0[0, inner] = ux_in[...]
             for i, field in enumerate((fv0, fv1, fv2)):
                 field[0, inner] = vx_in[i, 0]
                 field[NXL + 1, inner] = vx_in[i, 1]
             for x in range(NXL):
                 lrow = pl.ds(x, 1)
+                fu1[x + 1, pl.ds(TOP - 1, 1)] = uy_in[lrow]
                 fp[x + 1, pl.ds(TOP - 1, 1)] = pyup_in[lrow]
                 fp[x + 1, pl.ds(LAST + 1, 1)] = pydn_in[lrow]
                 for i, field in enumerate((fv0, fv1, fv2)):
@@ -484,7 +654,7 @@
                     r = TOP + 8 * k
                     rows, own = pl.ds(r, 8), pl.ds(8 * k, 8)
                     p = fp[x + 1, rows]
-                    pe = place(x, k, zmix[1])
+                    pe = place(x, k, zmix[0])
                     gu = (
                         -0.5 * (fp[x + 2, rows] - p),
                         -0.5 * (fp[x + 1, pl.ds(r + 1, 8)] - p),
@@ -499,7 +669,7 @@
                     bases[0, x, own] = (
                         (gd[0] * fu0[x, rows] + gu[0] * fu0[x + 1, rows])
                         + (gd[1] * fu1[x + 1, pl.ds(r - 1, 8)] + gu[1] * fu1[x + 1, rows])
-                        + (gd[2] * below(u2, place(x, k, zmix[2])) + gu[2] * u2)
+                        + (gd[2] * below(u2, place(x, k, zmix[1])) + gu[2] * u2)
                     )
                     for i, field in enumerate((fv0, fv1, fv2)):
                         v, up, down = around(x, k, i, field)
@@ -596,6 +766,7 @@
     block = pltpu.VMEM((NXL, NYL, NZL), F32)
     flat = pltpu.VMEM((NXL, NZL), F32)
     flats = pltpu.VMEM((3, NXL, NZL), F32)
+    pair = pltpu.VMEM((2, NXL, NZL), F32)
     tile = pltpu.VMEM((8, NZL), F32)
     tiles = pltpu.VMEM((3, 8, NZL), F32)
     dma = pltpu.SemaphoreType.DMA
@@ -617,25 +788,37 @@
             pltpu.VMEM((NXL, NYL, NZL), jnp.int32),
             *[field] * 8,
             pltpu.VMEM((NXL + 1, NYL, NZL), F32),
-            *[block] * 5,
-            pltpu.VMEM((2, NXL, NZL), F32),
+            *[block] * 4,
+            pair,
             *[block] * 4,
             pltpu.VMEM((3, 3, NXL, NYL, NZL), F32),
             pltpu.VMEM((4, NXL, NYL, NZL), F32),
-            pltpu.VMEM((2, NXL, NZL), F32), flat, pltpu.VMEM((2, NXL, NZL), F32), flat,
+            *[pltpu.VMEM((2, 2 * NYL + 8, NZL), F32)] * 2,
+            *[pltpu.VMEM((2, 2 * NXL + 8, NZL), F32)] * 2,
+            *[tiles] * 3,
+            *[pltpu.VMEM((2, NYL, NZL), F32)] * 2,
+            *[pair] * 2,
+            *[tile] * 3,
+            pltpu.VMEM((4, NXL, NZL), F32),
+            pltpu.VMEM((4, 8, NZL), F32),
+            pltpu.VMEM((4, 8, NZL), F32),
+            pltpu.VMEM((4, NXL, NZL), F32),
+            *[flat] * 3,
+            pltpu.VMEM((2, NYL, NZL), F32), pltpu.VMEM((NYL, NZL), F32), pair, flat,
             *[flat] * 4,
             *[flats] * 2,
             pltpu.VMEM((3, 2, NXL, NZL), F32),
             pltpu.VMEM((3, 2, NYL, NZL), F32),
-            *[pltpu.VMEM((2, 8, NZL), F32)] * 3,
-            *[tile] * 3,
-            *[tiles] * 5,
+            *[tile] * 8,
+            pltpu.VMEM((2, 8, NZL), F32),
+            *[tiles] * 4,
             pltpu.VMEM((sum(RING ** len(axes) for axes in PHASES), 1, NZL), F32),
             dma((5,)),
-            dma((13,)), dma((13,)), dma((3, 6)), dma((3, 6)),
+            dma((15,)), dma((15,)), dma((3, 6)), dma((3, 6)),
             dma((len(PHASES),)), dma((len(PHASES),)),
             pltpu.SemaphoreType.REGULAR,
             pltpu.SemaphoreType.REGULAR((3, 3)),
+            dma((28,)), dma((28,)),
         ],
         compiler_params=pltpu.CompilerParams(
             collective_id=0, has_side_effects=True, vmem_limit_bytes=24 * 1024 * 1024

time: 42.4 us -> 40.3 us (0.950)
  Pallas kernels: 41.6 us -> 39.6 us
    pallas_call x1, Pallas kernels: 40.7 us -> 38.6 us  [on_device(): pl.pallas_call(body, out_shape=out_shape, in_specs=[in_hbm] * 3, out_spec...]
where the time goes in v4:
time: 40.3 us; the launch traced here: 40.2 us
  Pallas kernels  39.6 us (98%)
  between operations  0.64 us (2%)
    pallas_call x1, Pallas kernels, on_device(): pl.pallas_call(body, out_shape=out_shape, in_specs=[in_hbm] * 3, out_spec...  38.6 us
    pallas_call x1, Pallas kernels, on_device(): pl.pallas_call(save, out_shape=out_shape, in_specs=[in_vmem] * 2, out_spe...  0.98 us

profile of v4, /device:TPU:1, one launch (start us, length us, event | category | flops | bytes accessed | tf_op | source)
XLA Modules:
  0.0 40.2 jit_solution(10700503433091564199)
XLA Ops:
  0.6 38.6 %projection_adjoint.1 = (f32[3,16,32,128]{3,2,1,0:T(8,128)S(1)}, f32[16,32,128]{2,1,0:T(8,128)S(1)}) custom-call(s32[16,32,128]{2,1,0:T(8,128)} %mask_hbm.1, f32[16,32,128]{2,1,0:T(8,128)} %press_hbm.1, f32[3,16,32,128]{3,2,1,0:T(8,128)} %vel_hbm.1), custom_call_target="tpu_custom_call" | custom-call | tf_op jit(solution)/shard_map/projection_adjoint/pallas_call | solution.py:782
  39.2 1.0 %save.1 = (f32[3,16,32,128]{3,2,1,0:T(8,128)}, f32[16,32,128]{2,1,0:T(8,128)}) custom-call(f32[3,16,32,128]{3,2,1,0:T(8,128)S(1)} %get-tuple-element.4.ustar, f32[16,32,128]{2,1,0:T(8,128)S(1)} %get-tuple-element.5.coef), custom_call_target="tpu_custom_call" | custom-call | tf_op jit(solution)/shard_map/save/pallas_call | solution.py:828

commit v5 on v4

--- a/solution.py
+++ b/solution.py
@@ -155,6 +155,14 @@
     plane = jnp.zeros((NYL, NZL), F32)
     line = jnp.zeros((1, NZL), F32)
     zero = jnp.zeros((8, NZL), F32)
+    for buffer in (ux_in, cy_in, uy_in, cz_lo, cz_hi, uz_lo):
+        buffer[...] = jnp.zeros(buffer.shape, F32)
+    cx_in[...] = jnp.full(cx_in.shape, 3, jnp.int32)
+
+    barrier = pltpu.get_barrier_semaphore()
+    for axis in AXES:
+        for other in (fwd[axis], bwd[axis]):
+            pl.semaphore_signal(barrier, inc=1, device_id={axis: other}, device_id_type=MESH)
     for field in (fc, fp, fu0, fv0, fv1, fv2):
         field[0, inner] = plane
         field[NXL + 1, inner] = plane
@@ -164,16 +172,12 @@
             field[x, pl.ds(TOP - 1, 1)] = line
             field[x, pl.ds(LAST + 1, 1)] = line
     for buffer in (
-        cx_in, ux_in, cy_in, uy_in, pyup_in, pydn_in, vy_in, vx_in,
-        cz_lo, cz_hi, uz_lo, pz_lo, pz_hi, vz_lo, vz_hi,
+        pyup_in, pydn_in, vy_in, vx_in,
+        pz_lo, pz_hi, vz_lo, vz_hi,
         kx_in, ky_in, kz_lo, kz_hi, tx_in, ty_in, tz_lo, tz_hi, dxy, dxz, dyz, dyz_rows, kx_out, ky_out,
     ):
         buffer[...] = jnp.zeros(buffer.shape, F32)
 
-    barrier = pltpu.get_barrier_semaphore()
-    for axis in AXES:
-        for other in (fwd[axis], bwd[axis]):
-            pl.semaphore_signal(barrier, inc=1, device_id={axis: other}, device_id_type=MESH)
     def pick(x, k, value, packed):
         return jnp.where(half == BLOCKS * x + k, roll(value, 2 * BLOCKS * x + 2 * k + 1, 1), packed)
 
@@ -186,12 +190,29 @@
     def below(value, edge):
         return jnp.where(first, edge, roll(value, 1, 1))
 
+    pl.semaphore_wait(barrier, 6)
+    sent = []
+
+    def launch(copies):
+        for copy in copies:
+            copy.start()
+        sent.extend(copies)
+        return copies
+
+    round1 = launch([
+        Shift(mask_hbm.at[NXL - 1], cx_in.at[0], send1.at[0], recv1.at[0], "gx", True),
+        Shift(mask_hbm.at[0], cx_in.at[1], send1.at[1], recv1.at[1], "gx", False),
+        Shift(vel_hbm.at[0, NXL - 1], ux_in, send1.at[7], recv1.at[7], "gx", True),
+    ])
     loads[0].wait()
 
+    def coefficient(phase):
+        c = jnp.where(phase == 0, 8.0, jnp.where(phase == 1, 1.0, jnp.where(phase == 2, 2.0, 0.0)))
+        return c.astype(F32)
+
     def prepare(x, packed):
         for k in range(BLOCKS):
-            phase = mask[x, pl.ds(8 * k, 8)]
-            c = jnp.where(phase == 0, 8.0, jnp.where(phase == 1, 1.0, 2.0)).astype(F32)
+            c = coefficient(mask[x, pl.ds(8 * k, 8)])
             fc[x + 1, pl.ds(TOP + 8 * k, 8)] = c
             packed = pick(x, k, c, packed)
             if k == 0:
@@ -201,22 +222,11 @@
         return packed
 
     cz[...] = lax.fori_loop(0, NXL, prepare, zero, unroll=4)
-    pl.semaphore_wait(barrier, 6)
-    sent = []
-
-    def launch(copies):
-        for copy in copies:
-            copy.start()
-        sent.extend(copies)
-        return copies
-
-    round1 = launch([
-        Shift(fc.at[NXL, inner], cx_in.at[0], send1.at[0], recv1.at[0], "gx", True),
-        Shift(fc.at[1, inner], cx_in.at[1], send1.at[1], recv1.at[1], "gx", False),
+    round1 += launch([
+        Shift(cz, cz_lo, send1.at[4], recv1.at[4], "gz", True),
+        Shift(cz, cz_hi, send1.at[5], recv1.at[5], "gz", False),
         Shift(cyup, cy_in.at[0], send1.at[2], recv1.at[2], "gy", True),
         Shift(cydn, cy_in.at[1], send1.at[3], recv1.at[3], "gy", False),
-        Shift(cz, cz_lo, send1.at[4], recv1.at[4], "gz", True),
-        Shift(cz, cz_hi, send1.at[5], recv1.at[5], "gz", False),
     ])
     for load in loads[1:4]:
         load.wait()
@@ -230,7 +240,6 @@
     uz[...] = lax.fori_loop(0, NXL, velocity, zero, unroll=4)
     round1 += launch([
         Shift(uz, uz_lo, send1.at[6], recv1.at[6], "gz", True),
-        Shift(fu0.at[NXL, inner], ux_in, send1.at[7], recv1.at[7], "gx", True),
         Shift(uyup, uy_in, send1.at[8], recv1.at[8], "gy", True),
     ])
     tell(0)
@@ -285,12 +294,12 @@
     for copy in round1:
         copy.wait_recv()
 
-    h = 0.5 * cx_in[0]
+    h = 0.5 * coefficient(cx_in[0])
     w = 0.5 * fc[1, inner] + h
     wx[0] = w
     minv[0] = minv[0] + h
     rhs[0] = rhs[0] - w * ux_in[...]
-    h = 0.5 * cx_in[1]
+    h = 0.5 * coefficient(cx_in[1])
     wx[NXL] = wx[NXL] + h
     minv[NXL - 1] = minv[NXL - 1] + h
     rhs[NXL - 1] = rhs[NXL - 1] + h * fu0[NXL, inner]
@@ -628,7 +637,7 @@
         offsets = [()]
         for axis in axes:
             offsets = [o + (d,) for o in offsets for d in range(RING)]
-        offsets = sorted(offsets[1:], key=lambda o: -sum(min(d, RING - d) for d in o))
+        offsets = sorted(offsets[1:], key=lambda o: urgency(o))
         for o in offsets:
             device = {axis: lax.rem(pos[axis] + d, RING) for axis, d in zip(axes, o) if d}
             remote(slots.at[mine], slots.at[mine], sendr.at[phase], recvr.at[phase], device).start()
@@ -727,6 +736,13 @@
     if width == 4:
         return roll(x, 4, 0)
     return jnp.where(keep, roll(x, 8 - width, 0), roll(x, width, 0))
+
+
+def urgency(offset):
+    steps = [min(d, RING - d) for d in offset]
+    if len(offset) == 1:
+        return -steps[0]
+    return (offset[0] + RING - 1) % RING + (RING // 2 - steps[1]) - 0.75 * sum(steps)
 
 
 def sum_tree(values):
@@ -804,7 +820,7 @@
             pltpu.VMEM((4, 8, NZL), F32),
             pltpu.VMEM((4, NXL, NZL), F32),
             *[flat] * 3,
-            pltpu.VMEM((2, NYL, NZL), F32), pltpu.VMEM((NYL, NZL), F32), pair, flat,
+            pltpu.VMEM((2, NYL, NZL), jnp.int32), pltpu.VMEM((NYL, NZL), F32), pair, flat,
             *[flat] * 4,
             *[flats] * 2,
             pltpu.VMEM((3, 2, NXL, NZL), F32),

time: 40.3 us -> 40.6 us (level)
  no operation moved by 1% of the time
where the time goes in v5:
time: 40.6 us; the launch traced here: 40.5 us
  Pallas kernels  39.8 us (98%)
  between operations  0.64 us (2%)
    pallas_call x1, Pallas kernels, on_device(): pl.pallas_call(body, out_shape=out_shape, in_specs=[in_hbm] * 3, out_spec...  38.8 us
    pallas_call x1, Pallas kernels, on_device(): pl.pallas_call(save, out_shape=out_shape, in_specs=[in_vmem] * 2, out_spe...  0.98 us

profile of v5, /device:TPU:1, one launch (start us, length us, event | category | flops | bytes accessed | tf_op | source)
XLA Modules:
  0.0 40.5 jit_solution(3259115507292260133)
XLA Ops:
  0.6 38.8 %projection_adjoint.1 = (f32[3,16,32,128]{3,2,1,0:T(8,128)S(1)}, f32[16,32,128]{2,1,0:T(8,128)S(1)}) custom-call(s32[16,32,128]{2,1,0:T(8,128)} %mask_hbm.1, f32[16,32,128]{2,1,0:T(8,128)} %press_hbm.1, f32[3,16,32,128]{3,2,1,0:T(8,128)} %vel_hbm.1), custom_call_target="tpu_custom_call" | custom-call | tf_op jit(solution)/shard_map/projection_adjoint/pallas_call | solution.py:798
  39.5 1.0 %save.1 = (f32[3,16,32,128]{3,2,1,0:T(8,128)}, f32[16,32,128]{2,1,0:T(8,128)}) custom-call(f32[3,16,32,128]{3,2,1,0:T(8,128)S(1)} %get-tuple-element.4.ustar, f32[16,32,128]{2,1,0:T(8,128)S(1)} %get-tuple-element.5.coef), custom_call_target="tpu_custom_call" | custom-call | tf_op jit(solution)/shard_map/save/pallas_call | solution.py:844
